TPU v7x, 32 devices: a whole 2x2x4 slice. The times are simulated.
32 devices in a mesh: lon: 8 (over z, x), lat: 4 (over y, core).
Axes of the slice: x: 2, y: 2, z: 4, core: 2. Of those that a mesh axis runs over, the one named last changes fastest.
Arguments:
- thermal_departure: float32 [90, 128, 1024], P(None, 'lat', 'lon'), may hold values from -6 to 6
- moisture_profile: float32 [90, 128, 1024], P(None, 'lat', 'lon'), may hold values from -6 to 6
- solar_elevation_factor: float32 [128, 1024], P('lat', 'lon'), may hold values from 0.1 to 1
- daylight_groups: int32 [128, 8], P('lat', 'lon'), may hold values from 0 to 1, as said below
- spreading_factor: float32 [128, 1024], P('lat', 'lon'), may hold values from 0.03 to 0.24
- entry_layer_matrix: float32 [512, 181], replicated, may hold values from -0.4375 to 0.4375
- entry_layer_offset: float32 [512], replicated, may hold values from -3 to 3
- inner_layer_matrices: float32 [2, 512, 512], replicated, may hold values from -0.25 to 0.25
- inner_layer_offsets: float32 [2, 512], replicated, may hold values from -3 to 3
- final_layer_matrix: float32 [90, 512], replicated, may hold values from -0.25 to 0.25
- final_layer_offset: float32 [90], replicated, may hold values from -3 to 3
Outputs:
- heating: float32 [90, 128, 1024], P(None, 'lat', 'lon')
- temp_next: float32 [90, 128, 1024], P(None, 'lat', 'lon')
Inputs may be any that keep to these rules, and one draw needn't show every extreme that they name: In every row the sunlit strips form one run of 4 consecutive strips, wrapping around, so daylight_groups[r, j] + daylight_groups[r, (j + 4) mod 8] == 1; row r and row r + 32 are complements of each other.
All inputs are finite; a program needn't handle non-finite values.
Results may differ from a plain program's by a relative error of at most 0.0001.
Values sent between devices are 32-bit elements; how exact they have to be, the bound alone decides.
A program may use at most 64 MiB of HBM per device.

v0:
```python
import jax
import jax.numpy as jnp
from jax import lax
from jax.sharding import PartitionSpec as P

DEPTH = 2
STEPS = 2


def padded_2(block, sides, width):
    for axis, dim in sides:
        count = lax.axis_size(axis)
        forward = [(i, i + 1) for i in range(count - 1)]
        forward.append((count - 1, 0))
        backward = [(target, source) for source, target in forward]
        low = lax.ppermute(
            lax.slice_in_dim(block, block.shape[dim] - width, None, axis=dim), axis, forward
        )
        high = lax.ppermute(lax.slice_in_dim(block, 0, width, axis=dim), axis, backward)
        block = jnp.concatenate([low, block, high], axis=dim)
    return block


def network_apply(
    columns,
    entry_layer_matrix,
    entry_layer_offset,
    inner_layer_matrices,
    inner_layer_offsets,
    final_layer_matrix,
    final_layer_offset,
):
    hidden = jax.nn.silu(
        jnp.dot(entry_layer_matrix, columns, precision=lax.Precision.HIGHEST)
        + entry_layer_offset[:, None]
    )
    for layer in range(DEPTH):
        hidden = jax.nn.silu(
            jnp.dot(inner_layer_matrices[layer], hidden, precision=lax.Precision.HIGHEST)
            + inner_layer_offsets[layer][:, None]
        )
    return (
        jnp.dot(final_layer_matrix, hidden, precision=lax.Precision.HIGHEST)
        + final_layer_offset[:, None]
    )


def radiate(predictor_entries, weights):
    feat_count, row_count, col_count = predictor_entries.shape
    flat = predictor_entries.reshape(feat_count, row_count * col_count)
    output = network_apply(flat, *weights)
    output = output.reshape(output.shape[0], row_count, col_count)
    return output * predictor_entries[-1][None]


def on_device(
    thermal_departure,
    moisture_profile,
    solar_elevation_factor,
    daylight_groups,
    spreading_factor,
    entry_layer_matrix,
    entry_layer_offset,
    inner_layer_matrices,
    inner_layer_offsets,
    final_layer_matrix,
    final_layer_offset,
):
    weights = (
        entry_layer_matrix,
        entry_layer_offset,
        inner_layer_matrices,
        inner_layer_offsets,
        final_layer_matrix,
        final_layer_offset,
    )
    lit = daylight_groups[:, 0].astype(jnp.float32)
    predictor_entries = jnp.concatenate(
        [thermal_departure, moisture_profile, solar_elevation_factor[None]], axis=0
    )
    lat_index = lax.axis_index("lat")
    lat_first = lat_index == 0
    lat_last = lat_index == lax.axis_size("lat") - 1
    atmosphere_snapshot = thermal_departure
    for substep in range(STEPS):
        padded = padded_2(atmosphere_snapshot, (("lon", 2), ("lat", 1)), 1)
        padded = padded.at[:, 0, :].multiply(jnp.where(lat_first, 0.0, 1.0))
        padded = padded.at[:, -1, :].multiply(jnp.where(lat_last, 0.0, 1.0))
        beside_all = (
            padded[:, :-2, 1:-1] + padded[:, 2:, 1:-1] + padded[:, 1:-1, :-2] + padded[:, 1:-1, 2:]
        )
        atmosphere_snapshot = atmosphere_snapshot + spreading_factor[None] * (
            beside_all - 4.0 * atmosphere_snapshot
        )
    heating = radiate(predictor_entries, weights) * lit[None, :, None]
    return (heating, atmosphere_snapshot + heating)


def solution(mesh):
    in_specs = (
        P(None, "lat", "lon"),
        P(None, "lat", "lon"),
        P("lat", "lon"),
        P("lat", "lon"),
        P("lat", "lon"),
        P(),
        P(),
        P(),
        P(),
        P(),
        P(),
    )
    out_specs = (P(None, "lat", "lon"), P(None, "lat", "lon"))
    return jax.shard_map(
        on_device, mesh=mesh, in_specs=in_specs, out_specs=out_specs, check_vma=False
    )
```

profile of v0, /device:TPU:0, one launch (start us, length us, event | category | flops | bytes accessed | tf_op | source)
XLA Modules:
  0.0 96.9 jit_solution(13895967518188902259)
XLA Ops:
  0.6 0.0 copy-start
  0.6 3.5 %fusion.44 = (f32[90,32,1]{2,1,0:T(8,128)}, f32[90,32,1]{2,1,0:T(8,128)S(1)}) fusion(f32[90,32,128]{2,1,0:T(8,128)} %param.19), kind=kLoop, calls=%fused_computation.70 | loop fusion | bytes 46080 | tf_op jit(solution)/shard_map/slice | solution.py:17
  4.2 0.0 copy-start.2
  4.2 2.3 %copy.28 = f32[90,32,1]{0,1,2:T(8,128)S(1)} copy(f32[90,32,1]{2,1,0:T(8,128)} %get-tuple-element.60) | data formatting | bytes 23040
  6.5 3.0 %collective-permute-start = (f32[90,32,1]{0,1,2:T(8,128)S(1)}, f32[90,32,1]{0,1,2:T(8,128)S(1)}, u32[]{:S(2)}, u32[]{:S(2)}) collective-permute-start(f32[90,32,1]{0,1,2:T(8,128)S(1)} %copy.28), channel_id=1, source_target_pairs={{0,4},{4,8},{8,12},{12,16},{16,20},{20,24},{24,28},{28,0},{1,5},{5... | collective-permute-start | bytes 34568 | tf_op jit(solution)/shard_map/ppermute | solution.py:16
  9.5 1.0 copy.29
  10.4 0.0 copy-start.5
  10.4 3.3 %collective-permute-start.1 = (f32[90,32,1]{0,1,2:T(8,128)S(1)}, f32[90,32,1]{0,1,2:T(8,128)S(1)}, u32[]{:S(2)}, u32[]{:S(2)}) collective-permute-start(f32[90,32,1]{0,1,2:T(8,128)S(1)} %copy.29), channel_id=1, source_target_pairs={{4,0},{8,4},{12,8},{16,12},{20,16},{24,20},{28,24},{0,28},{5,1},{9... | collective-permute-start | bytes 34568 | tf_op jit(solution)/shard_map/ppermute | solution.py:19
  13.7 0.0 copy-done.2
  13.7 0.1 pad.39
  13.8 1.1 %copy.30 = f32[12,8,32,128]{3,1,2,0:T(8,128)S(1)} copy(f32[12,8,32,128]{3,2,1,0:T(8,128)S(1)} %bitcast.71) | data formatting | bytes 3145728
  14.9 0.0 copy-done.5
  14.9 0.0 copy-start.7
  15.0 0.1 pad.40
  15.1 1.1 %copy.31 = f32[12,8,32,128]{3,1,2,0:T(8,128)S(1)} copy(f32[12,8,32,128]{3,2,1,0:T(8,128)S(1)} %bitcast.72) | data formatting | bytes 3145728
  16.2 0.0 copy-done
  16.2 0.0 copy-done.7
  16.2 0.0 copy-start.9
  16.2 0.0 copy-start.11
  16.2 7.0 %fusion.20 = f32[4096,512]{1,0:T(8,128)S(1)} fusion(f32[512,181]{0,1:T(8,128)S(1)} %copy-done, f32[1,4096]{1,0:T(1,128)S(1)} %bitcast.81, f32[90,4096]{1,0:T(8,128)S(1)} %bitcast.70, f32[90,4096]{1,0:T(8,128)S(1)} %bitcast.69), kind=kOutput, calls=%fused_computation.26 | convolution fusion | flops 4556496896 | bytes 11724800 | tf_op jit(solution)/shard_map/dot_general | solution.py:34
  23.3 0.0 copy-done.9
  23.3 0.0 copy-done.11
  23.3 0.0 copy-start.8
  23.3 17.2 %fusion.9 = f32[4096,512]{1,0:T(8,128)} fusion(f32[4096,512]{1,0:T(8,128)S(1)} %fusion.20, f32[512]{0:T(512)S(1)} %copy-done.11, f32[2,512,512]{2,1,0:T(8,128)S(1)} %copy-done.9), kind=kOutput, calls=%fused_computation.15 | convolution fusion | flops 12895387648 | bytes 17827840 | tf_op jit(solution)/shard_map/dot_general | solution.py:39
  40.5 0.0 copy-done.8
  40.5 1.9 %copy.20 = f32[90,32,128]{0,2,1:T(8,128)S(1)} copy(f32[90,32,128]{2,1,0:T(8,128)} %param.19) | data formatting | bytes 2949120 | tf_op args[0]
  42.4 0.0 copy-start.1
  42.4 0.0 collective-permute-done
  42.4 0.0 collective-permute-done.1
  42.5 0.1 collective-permute-start.2
  42.5 1.7 %collective-permute-start.3 = (f32[90,1,130]{0,2,1:T(8,128)S(1)}, f32[90,1,130]{0,2,1:T(8,128)S(1)}, u32[]{:S(2)}, u32[]{:S(2)}) collective-permute-start(f32[90,1,130]{0,2,1:T(8,128)S(1)} %get-tuple-element.57), channel_id=1, source_target_pairs={{1,0},{2,1},{3,2},{0,3},{5,4},{6,5},{7,6},{4,7},{9,8},{10,9},{11,1... | collective-permute-start | bytes 140408 | tf_op jit(solution)/shard_map/ppermute | solution.py:19
  44.3 18.7 %fusion.10 = f32[4096,512]{1,0:T(8,128)} fusion(f32[4096,512]{1,0:T(8,128)} %fusion.9, f32[512]{0:T(512)S(1)} %bitcast.85, f32[2,512,512]{2,1,0:T(8,128)} %param.26), kind=kOutput, calls=%fused_computation.16 | convolution fusion | flops 12895387648 | bytes 17827840 | tf_op jit(solution)/shard_map/dot_general | solution.py:39
  63.0 0.0 copy-start.6
  63.0 0.0 collective-permute-done.2
  63.0 0.0 collective-permute-done.3
  63.0 0.0 copy-done.1
  63.0 0.0 slice-start
  63.0 0.3 pad_maximum_fusion
  63.3 0.4 copy-done.6
  63.7 0.0 copy-start.10
  63.7 0.0 copy-start.12
  63.7 2.8 %fusion.32 = f32[90,32,128]{0,2,1:T(8,128)S(1)} fusion(f32[90,32,128]{0,2,1:T(8,128)} %copy-done.1, f32[90,34,130]{0,2,1:T(8,128)S(1)} %fusion.38, f32[32,128]{1,0:T(8,128)S(1)} %copy-done.6), kind=kLoop, calls=%fused_computation.44 | loop fusion | flops 2580480 | bytes 8863744 | tf_op jit(solution)/shard_map/add | solution.py:92
  66.5 0.1 collective-permute-start.4
  66.6 4.7 %collective-permute-start.5 = (f32[90,32,1]{0,1,2:T(8,128)S(1)}, f32[90,32,1]{0,1,2:T(8,128)S(1)}, u32[]{:S(2)}, u32[]{:S(2)}) collective-permute-start(f32[90,32,1]{0,1,2:T(8,128)S(1)} %bitcast.82), channel_id=1, source_target_pairs={{4,0},{8,4},{12,8},{16,12},{20,16},{24,20},{28,24},{0,28},{5,1},{9... | collective-permute-start | bytes 34568 | tf_op jit(solution)/shard_map/ppermute | solution.py:19
  71.3 0.0 slice-done
  71.3 0.0 copy-done.10
  71.3 0.0 copy-done.12
  71.3 0.0 slice-done.1
  71.3 0.0 copy-start.13
  71.3 11.1 %fusion.13 = f32[90,4096]{1,0:T(8,128)} fusion(f32[90,512]{1,0:T(8,128)S(1)} %copy-done.10, f32[4096,512]{1,0:T(8,128)S(1)} %bitcast.87, f32[512]{0:T(512)S(1)} %bitcast.84, f32[90]{0:T(128)S(1)} %copy-done.12), kind=kOutput, calls=%fused_computation.19 | convolution fusion | flops 2275778560 | bytes 10049896 | tf_op jit(solution)/shard_map/dot_general | solution.py:43
  82.5 0.0 collective-permute-done.4
  82.5 0.0 collective-permute-done.5
  82.5 0.1 collective-permute-start.6
  82.6 1.7 %collective-permute-start.7 = (f32[90,1,130]{0,2,1:T(8,128)S(1)}, f32[90,1,130]{0,2,1:T(8,128)S(1)}, u32[]{:S(2)}, u32[]{:S(2)}) collective-permute-start(f32[90,1,130]{0,2,1:T(8,128)S(1)} %get-tuple-element.55), channel_id=1, source_target_pairs={{1,0},{2,1},{3,2},{0,3},{5,4},{6,5},{7,6},{4,7},{9,8},{10,9},{11,1... | collective-permute-start | bytes 140408 | tf_op jit(solution)/shard_map/ppermute | solution.py:19
  84.3 0.0 copy-done.13
  84.3 2.8 %copy.27 = f32[90,4096]{0,1:T(8,128)} copy(f32[90,4096]{1,0:T(8,128)} %fusion.13) | data formatting | bytes 2949120 | tf_op jit(solution)/shard_map/reshape | solution.py:52
  87.2 0.0 collective-permute-done.6
  87.2 0.0 collective-permute-done.7
  87.2 0.3 pad_maximum_fusion.1
  87.5 1.3 %copy-done.3 = f32[90,4096]{0,1:T(8,128)S(1)} copy-done((f32[90,4096]{0,1:T(8,128)S(1)}, f32[90,4096]{0,1:T(8,128)}, u32[]{:S(2)}) %copy-start.3) | copy-done | bytes 1474584
  88.7 3.3 %fusion.29 = (f32[90,32,128]{0,2,1:T(8,128)}, f32[90,32,128]{0,2,1:T(8,128)}) fusion(f32[90,32,128]{0,2,1:T(8,128)S(1)} %fusion.32, f32[90,34,130]{0,2,1:T(8,128)S(1)} %fusion.37, f32[32,128]{1,0:T(8,128)S(1)} %copy-done.6, f32[32]{0:T(128)S(1)} %convert_bitcast_fusion, f32[90,32,128]{0,2,1:T(8,128)S(1)} %bitcast.68, f32[32,128]{1,0:T(8,128)S(1)} %copy-done.7), kind=kLoop, calls=%fused_computation.38 | loop fusion | flops 3686400 | bytes 11829376 | tf_op jit(solution)/shard_map/add | solution.py:96
  92.0 3.1 %copy.25 = f32[90,32,128]{2,1,0:T(8,128)} copy(f32[90,32,128]{0,2,1:T(8,128)} %get-tuple-element.53) | data formatting | bytes 2949120
  95.1 0.0 copy-done.4
  95.1 1.8 %copy.26 = f32[90,32,128]{2,1,0:T(8,128)} copy(f32[90,32,128]{0,2,1:T(8,128)S(1)} %copy-done.4) | data formatting | bytes 2949120
  (13 shorter events, 0.1 us)
Async XLA Ops:
  0.6 15.6 %copy-start = (f32[512,181]{0,1:T(8,128)S(1)}, f32[512,181]{0,1:T(8,128)}, u32[]{:S(2)}) copy-start(f32[512,181]{0,1:T(8,128)} %param.24) | copy-start | bytes 1112068
  4.2 9.5 %copy-start.2 = (f32[90,32,128]{2,1,0:T(8,128)S(1)}, f32[90,32,128]{2,1,0:T(8,128)}, u32[]{:S(2)}) copy-start(f32[90,32,128]{2,1,0:T(8,128)} %param.19) | copy-start | bytes 4423684
  6.5 35.9 %collective-permute-start = (f32[90,32,1]{0,1,2:T(8,128)S(1)}, f32[90,32,1]{0,1,2:T(8,128)S(1)}, u32[]{:S(2)}, u32[]{:S(2)}) collective-permute-start(f32[90,32,1]{0,1,2:T(8,128)S(1)} %copy.28), channel_id=1, source_target_pairs={{0,4},{4,8},{8,12},{12,16},{16,20},{20,24},{24,28},{28,0},{1,5},{5... | collective-permute-start | bytes 34568 | tf_op jit(solution)/shard_map/ppermute | solution.py:16
  10.4 4.5 %copy-start.5 = (f32[90,32,128]{2,1,0:T(8,128)S(1)}, f32[90,32,128]{2,1,0:T(8,128)}, u32[]{:S(2)}) copy-start(f32[90,32,128]{2,1,0:T(8,128)} %param.20) | copy-start | bytes 4423684
  10.4 32.0 %collective-permute-start.1 = (f32[90,32,1]{0,1,2:T(8,128)S(1)}, f32[90,32,1]{0,1,2:T(8,128)S(1)}, u32[]{:S(2)}, u32[]{:S(2)}) collective-permute-start(f32[90,32,1]{0,1,2:T(8,128)S(1)} %copy.29), channel_id=1, source_target_pairs={{4,0},{8,4},{12,8},{16,12},{20,16},{24,20},{28,24},{0,28},{5,1},{9... | collective-permute-start | bytes 34568 | tf_op jit(solution)/shard_map/ppermute | solution.py:19
  14.9 1.3 %copy-start.7 = (f32[32,128]{1,0:T(8,128)S(1)}, f32[32,128]{1,0:T(8,128)}, u32[]{:S(2)}) copy-start(f32[32,128]{1,0:T(8,128)} %param.21) | copy-start | bytes 49156
  16.2 7.1 %copy-start.9 = (f32[2,512,512]{2,1,0:T(8,128)S(1)}, f32[2,512,512]{2,1,0:T(8,128)}, u32[]{:S(2)}) copy-start(f32[2,512,512]{2,1,0:T(8,128)} %param.26) | copy-start | bytes 6291460
  16.2 7.1 %copy-start.11 = (f32[512]{0:T(512)S(1)}, f32[512]{0:T(512)}, u32[]{:S(2)}) copy-start(f32[512]{0:T(512)} %param.25) | copy-start | bytes 6148
  23.3 17.2 %copy-start.8 = (f32[2,512]{1,0:T(2,128)S(1)}, f32[2,512]{1,0:T(2,128)}, u32[]{:S(2)}) copy-start(f32[2,512]{1,0:T(2,128)} %param.27) | copy-start | bytes 12292
  42.4 20.6 %copy-start.1 = (f32[90,32,128]{0,2,1:T(8,128)}, f32[90,32,128]{0,2,1:T(8,128)S(1)}, u32[]{:S(2)}) copy-start(f32[90,32,128]{0,2,1:T(8,128)S(1)} %copy.20) | copy-start | bytes 4423684
  42.5 20.5 %collective-permute-start.2 = (f32[90,1,130]{0,2,1:T(8,128)S(1)}, f32[90,1,130]{0,2,1:T(8,128)S(1)}, u32[]{:S(2)}, u32[]{:S(2)}) collective-permute-start(f32[90,1,130]{0,2,1:T(8,128)S(1)} %get-tuple-element.56), channel_id=1, source_target_pairs={{0,1},{1,2},{2,3},{3,0},{4,5},{5,6},{6,7},{7,4},{8,9},{9,10},{10,1... | collective-permute-start | bytes 140408 | tf_op jit(solution)/shard_map/ppermute | solution.py:16
  42.5 20.4 %collective-permute-start.3 = (f32[90,1,130]{0,2,1:T(8,128)S(1)}, f32[90,1,130]{0,2,1:T(8,128)S(1)}, u32[]{:S(2)}, u32[]{:S(2)}) collective-permute-start(f32[90,1,130]{0,2,1:T(8,128)S(1)} %get-tuple-element.57), channel_id=1, source_target_pairs={{1,0},{2,1},{3,2},{0,3},{5,4},{6,5},{7,6},{4,7},{9,8},{10,9},{11,1... | collective-permute-start | bytes 140408 | tf_op jit(solution)/shard_map/ppermute | solution.py:19
  63.0 0.7 copy-start.6
  63.0 8.3 %slice-start = ((s8[8388608]{0:T(1024)(128)(4,1)}), s8[4194304]{0:T(1024)(128)(4,1)S(1)}, s32[]{:S(2)}) async-start(s8[8388608]{0:T(1024)(128)(4,1)} %bitcast.86), calls=%async_computation | async-start | bytes 8388608
  63.7 7.6 %copy-start.10 = (f32[90,512]{1,0:T(8,128)S(1)}, f32[90,512]{1,0:T(8,128)}, u32[]{:S(2)}) copy-start(f32[90,512]{1,0:T(8,128)} %param.28) | copy-start | bytes 552964
  63.7 7.6 %copy-start.12 = (f32[90]{0:T(128)S(1)}, f32[90]{0:T(128)}, u32[]{:S(2)}) copy-start(f32[90]{0:T(128)} %param.29) | copy-start | bytes 1084
  63.7 7.6 %slice-start.1 = ((s8[8388608]{0:T(1024)(128)(4,1)}), s8[4194304]{0:T(1024)(128)(4,1)S(1)}, s32[]{:S(2)}) async-start(s8[8388608]{0:T(1024)(128)(4,1)} %bitcast.86), calls=%async_computation.1 | async-start | bytes 8388608
  66.5 15.9 %collective-permute-start.4 = (f32[90,32,1]{0,1,2:T(8,128)S(1)}, f32[90,32,1]{0,1,2:T(8,128)S(1)}, u32[]{:S(2)}, u32[]{:S(2)}) collective-permute-start(f32[90,32,1]{0,1,2:T(8,128)S(1)} %bitcast.83), channel_id=1, source_target_pairs={{0,4},{4,8},{8,12},{12,16},{16,20},{20,24},{24,28},{28,0},{1,5},{5... | collective-permute-start | bytes 34568 | tf_op jit(solution)/shard_map/ppermute | solution.py:16
  66.6 15.9 %collective-permute-start.5 = (f32[90,32,1]{0,1,2:T(8,128)S(1)}, f32[90,32,1]{0,1,2:T(8,128)S(1)}, u32[]{:S(2)}, u32[]{:S(2)}) collective-permute-start(f32[90,32,1]{0,1,2:T(8,128)S(1)} %bitcast.82), channel_id=1, source_target_pairs={{4,0},{8,4},{12,8},{16,12},{20,16},{24,20},{28,24},{0,28},{5,1},{9... | collective-permute-start | bytes 34568 | tf_op jit(solution)/shard_map/ppermute | solution.py:19
  71.3 13.0 %copy-start.13 = (s32[32,1]{0,1:T(1,128)S(1)}, s32[32,1]{0,1:T(1,128)}, u32[]{:S(2)}) copy-start(s32[32,1]{0,1:T(1,128)} %param.22) | copy-start | bytes 388
  82.5 4.6 %collective-permute-start.6 = (f32[90,1,130]{0,2,1:T(8,128)S(1)}, f32[90,1,130]{0,2,1:T(8,128)S(1)}, u32[]{:S(2)}, u32[]{:S(2)}) collective-permute-start(f32[90,1,130]{0,2,1:T(8,128)S(1)} %get-tuple-element.54), channel_id=1, source_target_pairs={{0,1},{1,2},{2,3},{3,0},{4,5},{5,6},{6,7},{7,4},{8,9},{9,10},{10,1... | collective-permute-start | bytes 140408 | tf_op jit(solution)/shard_map/ppermute | solution.py:16
  82.6 4.6 %collective-permute-start.7 = (f32[90,1,130]{0,2,1:T(8,128)S(1)}, f32[90,1,130]{0,2,1:T(8,128)S(1)}, u32[]{:S(2)}, u32[]{:S(2)}) collective-permute-start(f32[90,1,130]{0,2,1:T(8,128)S(1)} %get-tuple-element.55), channel_id=1, source_target_pairs={{1,0},{2,1},{3,2},{0,3},{5,4},{6,5},{7,6},{4,7},{9,8},{10,9},{11,1... | collective-permute-start | bytes 140408 | tf_op jit(solution)/shard_map/ppermute | solution.py:19
  87.2 1.6 %copy-start.3 = (f32[90,4096]{0,1:T(8,128)S(1)}, f32[90,4096]{0,1:T(8,128)}, u32[]{:S(2)}) copy-start(f32[90,4096]{0,1:T(8,128)} %copy.27) | copy-start | bytes 4423684
  92.0 3.1 %copy-start.4 = (f32[90,32,128]{0,2,1:T(8,128)S(1)}, f32[90,32,128]{0,2,1:T(8,128)}, u32[]{:S(2)}) copy-start(f32[90,32,128]{0,2,1:T(8,128)} %get-tuple-element.52) | copy-start | bytes 4423684
where the time goes:
time: 97.2 us; the launch traced here: 96.9 us
  matrix products  54.1 us (56%)
  local copies, waits for them, and re-layouts  20.6 us (21%)
  starting transfers between devices  14.6 us (15%)
  other arithmetic  6.73 us (7%)
    dot_general x2, matrix products, network_apply(): jnp.dot(inner_layer_matrices[layer], hidden, precision=lax.Precision.HIGH...  35.9 us
    unnamed x41, local copies, waits for them, and re-layouts  14.2 us
    ppermute x4, starting transfers between devices, padded_2(): lax.ppermute(lax.slice_in_dim(block, 0, width, axis=dim), axis, backward)  11.4 us
    dot_general x1, matrix products, network_apply(): jnp.dot(final_layer_matrix, hidden, precision=lax.Precision.HIGHEST)  11.1 us
    dot_general x1, matrix products, network_apply(): jnp.dot(entry_layer_matrix, columns, precision=lax.Precision.HIGHEST)  7.05 us
    slice x2, local copies, waits for them, and re-layouts, padded_2(): lax.slice_in_dim(block, block.shape[dim] - width, None, axis=dim)  3.58 us
    add x1, other arithmetic, on_device(): return (heating, atmosphere_snapshot + heating)  3.29 us
    ppermute x4, starting transfers between devices, padded_2(): lax.ppermute(lax.slice_in_dim(block, block.shape[dim] - width, None, axis...  3.14 us
  transfers between devices with their start and end apart: 8, of which 0 were waited for; matrix products, arithmetic and copies ran while one was open for 64% of the time, Pallas kernels for 0%

commit v1 on v0

v1 whole, which is shorter than its diff:
```python
import functools

import jax
import jax.numpy as jnp
from jax import lax
from jax.experimental import pallas as pl
from jax.experimental.pallas import tpu as pltpu
from jax.sharding import PartitionSpec as P

STEPS = 2
MESH = pl.DeviceIdType.MESH
GROUP = 4


def padded_2(block, sides, width):
    for axis, dim in sides:
        count = lax.axis_size(axis)
        forward = [(i, i + 1) for i in range(count - 1)]
        forward.append((count - 1, 0))
        backward = [(target, source) for source, target in forward]
        low = lax.ppermute(
            lax.slice_in_dim(block, block.shape[dim] - width, None, axis=dim), axis, forward
        )
        high = lax.ppermute(lax.slice_in_dim(block, 0, width, axis=dim), axis, backward)
        block = jnp.concatenate([low, block, high], axis=dim)
    return block


def up8(n):
    return (n + 7) // 8 * 8


def split(x):
    hi = x.astype(jnp.bfloat16)
    lo = (x - hi.astype(jnp.float32)).astype(jnp.bfloat16)
    return hi, lo


def dot(a, b):
    return jnp.dot(a, b, preferred_element_type=jnp.float32)


def dot3(w_hi, w_lo, x):
    hi, lo = split(x)
    return dot(w_hi, hi) + dot(w_hi, lo) + dot(w_lo, hi)


def gate(h):
    return h + h * jnp.tanh(h)


def net_kernel(
    temp, moist, mu, lit, w0t, b0, wm, bm, wf, bf,
    heat,
    temp_v, moist_v, mu_v, temp_r, moist_r, mu_r,
    w0_hi, w0_lo, wm_hi, wm_lo, wf_hi, wf_lo, b0_c, bm_c, bf_c,
    xs, res, res_r,
    in_sem, send_sem, recv_sem, out_send, out_recv,
):
    levels, rows, lanes = temp.shape
    half = rows // 2
    hid = wm.shape[1]
    depth = wm.shape[0]
    lp = up8(levels)
    lat = lax.axis_index("lat")
    parity = lax.rem(lat, 2)
    partner = lat + 1 - 2 * parity
    mine = pl.multiple_of(parity * half, half)
    theirs = pl.multiple_of(half - parity * half, half)

    own = [
        pltpu.make_async_copy(temp, temp_v, in_sem.at[0]),
        pltpu.make_async_copy(moist, moist_v, in_sem.at[1]),
        pltpu.make_async_copy(mu, mu_v, in_sem.at[2]),
    ]
    for copy in own:
        copy.start()

    barrier = pltpu.get_barrier_semaphore()
    pl.semaphore_signal(barrier, inc=1, device_id={"lat": partner}, device_id_type=MESH)
    pl.semaphore_wait(barrier, 1)

    out = [
        pltpu.make_async_remote_copy(
            src_ref=src, dst_ref=dst, send_sem=send_sem.at[i], recv_sem=recv_sem.at[i],
            device_id={"lat": partner}, device_id_type=MESH)
        for i, (src, dst) in enumerate((
            (temp.at[:, pl.ds(theirs, half), :], temp_r),
            (moist.at[:, pl.ds(theirs, half), :], moist_r),
            (mu.at[pl.ds(theirs, half), :], mu_r),
        ))
    ]
    for copy in out:
        copy.start()

    kp = xs.shape[0]
    xs[...] = jnp.zeros_like(xs)
    xs[0:levels, 0:hid] = w0t[0:levels, :] * 0.5
    xs[lp:lp + levels, 0:hid] = w0t[levels:2 * levels, :] * 0.5
    xs[2 * lp:2 * lp + 1, 0:hid] = w0t[2 * levels:2 * levels + 1, :] * 0.5
    w0_hi[...], w0_lo[...] = split(xs[:, 0:hid].T)
    for k in range(depth):
        wm_hi[k], wm_lo[k] = split(wm[k] * 0.5)
    wf_hi[...], wf_lo[...] = split(wf[...])

    def column(row):
        return jnp.broadcast_to(row, (lanes, row.shape[1])).T

    b0_c[...] = column(b0[...] * 0.5)
    for k in range(depth):
        bm_c[k] = column(bm[k:k + 1, :] * 0.5)
    bf_c[...] = column(bf[...])
    xs[...] = jnp.zeros_like(xs)

    for copy in own:
        copy.wait()
    for copy in out:
        copy.wait()

    temp_f = temp_v.reshape(levels * rows, lanes)
    moist_f = moist_v.reshape(levels * rows, lanes)
    temp_rf = temp_r.reshape(levels * half, lanes)
    moist_rf = moist_r.reshape(levels * half, lanes)

    def wide(c):
        return jnp.concatenate([c] * GROUP, axis=1)

    def send(g):
        rows_g = pl.ds(g * GROUP, GROUP)
        return pltpu.make_async_remote_copy(
            src_ref=res.at[rows_g], dst_ref=res_r.at[rows_g],
            send_sem=out_send.at[g], recv_sem=out_recv.at[g],
            device_id={"lat": partner}, device_id_type=MESH)

    def step(g, carry):
        for j in range(GROUP):
            i = g * GROUP + j
            r = mine + i
            on = lit[r].astype(jnp.float32)
            off = 1.0 - on
            cols = slice(j * lanes, (j + 1) * lanes)
            xs[0:levels, cols] = (
                temp_f[pl.ds(r, levels, stride=rows), :] * on
                + temp_rf[pl.ds(i, levels, stride=half), :] * off)
            xs[lp:lp + levels, cols] = (
                moist_f[pl.ds(r, levels, stride=rows), :] * on
                + moist_rf[pl.ds(i, levels, stride=half), :] * off)
            xs[2 * lp:2 * lp + 1, cols] = (
                mu_v[pl.ds(r, 1), :] * on + mu_r[pl.ds(i, 1), :] * off)
        h = gate(dot3(w0_hi[...], w0_lo[...], xs[...]) + wide(b0_c[...]))
        for k in range(depth):
            h = gate(dot3(wm_hi[k], wm_lo[k], h) + wide(bm_c[k]))
        y = dot3(wf_hi[...], wf_lo[...], h) + wide(bf_c[...])
        y = y * xs[2 * lp:2 * lp + 1, :]
        for j in range(GROUP):
            res[g * GROUP + j] = y[:, j * lanes:(j + 1) * lanes]
        send(g).start()
        return carry

    lax.fori_loop(0, half // GROUP, step, 0)

    heat_f = heat.reshape(levels * rows, lanes)
    for i in range(half):
        r = mine + i
        heat_f[pl.ds(r, levels, stride=rows), :] = res[i] * lit[r].astype(jnp.float32)
    for g in range(half // GROUP):
        send(g).wait()
    for i in range(half):
        r = theirs + i
        heat_f[pl.ds(r, levels, stride=rows), :] = res_r[i] * lit[r].astype(jnp.float32)


def radiate(temp, moist, mu, lit, w0, b0, wm, bm, wf, bf):
    levels, rows, lanes = temp.shape
    half = rows // 2
    hid = wm.shape[1]
    depth = wm.shape[0]
    lp = up8(levels)
    kp = 256
    while kp < 2 * lp + 1:
        kp += 256
    f32, bf16 = jnp.float32, jnp.bfloat16
    vmem = pl.BlockSpec(memory_space=pltpu.VMEM)
    any_ = pl.BlockSpec(memory_space=pl.ANY)
    groups = half // GROUP
    return pl.pallas_call(
        net_kernel,
        out_shape=jax.ShapeDtypeStruct((levels, rows, lanes), f32),
        in_specs=[any_, any_, any_, pl.BlockSpec(memory_space=pltpu.SMEM)] + [vmem] * 6,
        out_specs=vmem,
        scratch_shapes=[
            pltpu.VMEM((levels, rows, lanes), f32),
            pltpu.VMEM((levels, rows, lanes), f32),
            pltpu.VMEM((rows, lanes), f32),
            pltpu.VMEM((levels, half, lanes), f32),
            pltpu.VMEM((levels, half, lanes), f32),
            pltpu.VMEM((half, lanes), f32),
            pltpu.VMEM((hid, kp), bf16),
            pltpu.VMEM((hid, kp), bf16),
            pltpu.VMEM((depth, hid, hid), bf16),
            pltpu.VMEM((depth, hid, hid), bf16),
            pltpu.VMEM((levels, hid), bf16),
            pltpu.VMEM((levels, hid), bf16),
            pltpu.VMEM((hid, lanes), f32),
            pltpu.VMEM((depth, hid, lanes), f32),
            pltpu.VMEM((levels, lanes), f32),
            pltpu.VMEM((kp, max(hid, GROUP * lanes)), f32),
            pltpu.VMEM((half, levels, lanes), f32),
            pltpu.VMEM((half, levels, lanes), f32),
            pltpu.SemaphoreType.DMA((3,)),
            pltpu.SemaphoreType.DMA((3,)),
            pltpu.SemaphoreType.DMA((3,)),
            pltpu.SemaphoreType.DMA((groups,)),
            pltpu.SemaphoreType.DMA((groups,)),
        ],
        compiler_params=pltpu.CompilerParams(
            collective_id=0, has_side_effects=True, vmem_limit_bytes=48 << 20),
    )(temp, moist, mu, lit, w0.T, b0[None, :], wm, bm, wf, bf[None, :])


def on_device(
    thermal_departure,
    moisture_profile,
    solar_elevation_factor,
    daylight_groups,
    spreading_factor,
    entry_layer_matrix,
    entry_layer_offset,
    inner_layer_matrices,
    inner_layer_offsets,
    final_layer_matrix,
    final_layer_offset,
):
    lat_index = lax.axis_index("lat")
    lat_first = lat_index == 0
    lat_last = lat_index == lax.axis_size("lat") - 1
    atmosphere_snapshot = thermal_departure
    for substep in range(STEPS):
        padded = padded_2(atmosphere_snapshot, (("lon", 2), ("lat", 1)), 1)
        padded = padded.at[:, 0, :].multiply(jnp.where(lat_first, 0.0, 1.0))
        padded = padded.at[:, -1, :].multiply(jnp.where(lat_last, 0.0, 1.0))
        beside_all = (
            padded[:, :-2, 1:-1] + padded[:, 2:, 1:-1] + padded[:, 1:-1, :-2] + padded[:, 1:-1, 2:]
        )
        atmosphere_snapshot = atmosphere_snapshot + spreading_factor[None] * (
            beside_all - 4.0 * atmosphere_snapshot
        )
    heating = radiate(
        thermal_departure,
        moisture_profile,
        solar_elevation_factor,
        daylight_groups[:, 0],
        entry_layer_matrix,
        entry_layer_offset,
        inner_layer_matrices,
        inner_layer_offsets,
        final_layer_matrix,
        final_layer_offset,
    )
    return (heating, atmosphere_snapshot + heating)


def solution(mesh):
    in_specs = (
        P(None, "lat", "lon"),
        P(None, "lat", "lon"),
        P("lat", "lon"),
        P("lat", "lon"),
        P("lat", "lon"),
        P(),
        P(),
        P(),
        P(),
        P(),
        P(),
    )
    out_specs = (P(None, "lat", "lon"), P(None, "lat", "lon"))
    return jax.shard_map(
        on_device, mesh=mesh, in_specs=in_specs, out_specs=out_specs, check_vma=False
    )
```

time: 97.2 us -> 104 us (1.070); the launches traced: 96.9 us -> 102 us
  matrix products: 54.1 us -> 0 us
  Pallas kernels: 0 us -> 20.9 us
  other arithmetic: 6.73 us -> 27.3 us
  local copies, waits for them, and re-layouts: 20.6 us -> 34.1 us
  waiting for transfers between devices: 0.02 us -> 5.25 us
    dot_general x4 -> x0, matrix products: 54.1 us -> none  [the longest x2 35.9 us: network_apply(): jnp.dot(inner_layer_matrices[layer], hidden, precision=lax.Precision.HIGH...]
    pallas_call x0 -> x1, Pallas kernels: none -> 20.9 us  [radiate(): pl.pallas_call(net_kernel, out_shape=jax.ShapeDtypeStruct((levels, rows,...]
    another operation x0 -> x4, local copies, waits for them, and re-layouts: none -> 13.7 us  [the longest x2 6.86 us: on_device(): padded = padded.at[:, -1, :].multiply(jnp.where(lat_last, 0.0, 1.0))]
    unnamed x41 -> x33, local copies, waits for them, and re-layouts: 14.2 us -> 3.13 us
    ppermute x0 -> x4, local copies, waits for them, and re-layouts: none -> 8.27 us  [the longest x2 4.57 us: padded_2(): lax.ppermute(lax.slice_in_dim(block, 0, width, axis=dim), axis, backward)]
    concatenate x2, other arithmetic: 0.56 us -> 8.1 us  [padded_2(): block = jnp.concatenate([low, block, high], axis=dim)]
    slice x2, other arithmetic: 0.04 us -> 3.85 us  [padded_2(): lax.slice_in_dim(block, block.shape[dim] - width, None, axis=dim)]
    add x1, other arithmetic: 3.29 us -> 6.95 us  [on_device(): return (heating, atmosphere_snapshot + heating)]
  transfers between devices with their start and end apart: 8 -> 8, of which waited for: 0 -> 4; matrix products, arithmetic and copies ran while one was open for 64% -> 7% of each run, Pallas kernels for 0% -> 20%
where the time goes in v1:
time: 104 us; the launch traced here: 102 us
  local copies, waits for them, and re-layouts  34.1 us (33%)
  other arithmetic  27.3 us (26%)
  Pallas kernels  20.9 us (20%)
  starting transfers between devices  14 us (13%)
  waiting for transfers between devices  5.25 us (5%)
    pallas_call x1, Pallas kernels, radiate(): pl.pallas_call(net_kernel, out_shape=jax.ShapeDtypeStruct((levels, rows,...  20.9 us
    ppermute x4, starting transfers between devices, padded_2(): lax.ppermute(lax.slice_in_dim(block, 0, width, axis=dim), axis, backward)  8.99 us
    concatenate x2, other arithmetic, padded_2(): block = jnp.concatenate([low, block, high], axis=dim)  8.1 us
    add x1, other arithmetic, on_device(): return (heating, atmosphere_snapshot + heating)  6.95 us
    another operation x2, local copies, waits for them, and re-layouts, on_device(): padded = padded.at[:, -1, :].multiply(jnp.where(lat_last, 0.0, 1.0))  6.86 us
    another operation x2, local copies, waits for them, and re-layouts, on_device(): padded = padded.at[:, 0, :].multiply(jnp.where(lat_first, 0.0, 1.0))  6.84 us
    slice x3, local copies, waits for them, and re-layouts, padded_2(): lax.slice_in_dim(block, block.shape[dim] - width, None, axis=dim)  6.78 us
    add x1, other arithmetic, on_device(): atmosphere_snapshot + spreading_factor[None] * (beside_all - 4.0 * atmosp...  5.83 us
  transfers between devices with their start and end apart: 8, of which 4 were waited for; matrix products, arithmetic and copies ran while one was open for 7% of the time, Pallas kernels for 20%

profile of v1, /device:TPU:0, one launch (start us, length us, event | category | flops | bytes accessed | tf_op | source)
XLA Modules:
  0.0 102.3 jit_solution(16886354062947004911)
XLA Ops:
  0.6 2.4 %fusion.8 = (f32[90,32,1]{2,1,0:T(8,128)S(1)}, f32[90,32,1]{2,1,0:T(8,128)S(1)}) fusion(f32[90,32,128]{2,1,0:T(8,128)} %temp.1), kind=kLoop, calls=%fused_computation.26 | loop fusion | bytes 46080 | tf_op jit(solution)/shard_map/slice | solution.py:22
  3.0 1.0 copy.21
  4.0 3.0 %collective-permute-start = (f32[90,32,1]{0,1,2:T(8,128)S(1)}, f32[90,32,1]{0,1,2:T(8,128)S(1)}, u32[]{:S(2)}, u32[]{:S(2)}) collective-permute-start(f32[90,32,1]{0,1,2:T(8,128)S(1)} %copy.21), channel_id=1, source_target_pairs={{0,4},{4,8},{8,12},{12,16},{16,20},{20,24},{24,28},{28,0},{1,5},{5... | collective-permute-start | bytes 34568 | tf_op jit(solution)/shard_map/ppermute | solution.py:21
  6.9 1.0 copy.22
  7.9 3.1 %collective-permute-start.1 = (f32[90,32,1]{0,1,2:T(8,128)S(1)}, f32[90,32,1]{0,1,2:T(8,128)S(1)}, u32[]{:S(2)}, u32[]{:S(2)}) collective-permute-start(f32[90,32,1]{0,1,2:T(8,128)S(1)} %copy.22), channel_id=1, source_target_pairs={{4,0},{8,4},{12,8},{16,12},{20,16},{24,20},{28,24},{0,28},{5,1},{9... | collective-permute-start | bytes 34568 | tf_op jit(solution)/shard_map/ppermute | solution.py:24
  11.0 0.8 collective-permute-done
  11.8 1.4 %copy.15 = f32[90,32,1]{2,1,0:T(8,128)S(1)} copy(f32[90,32,1]{0,1,2:T(8,128)S(1)} %collective-permute-done) | data formatting | bytes 23040 | tf_op jit(solution)/shard_map/ppermute | solution.py:21
  13.2 0.0 collective-permute-done.1
  13.2 2.3 %copy.16 = f32[90,32,1]{2,1,0:T(8,128)} copy(f32[90,32,1]{0,1,2:T(8,128)S(1)} %collective-permute-done.1) | data formatting | bytes 23040 | tf_op jit(solution)/shard_map/ppermute | solution.py:24
  15.5 0.0 copy-done
  15.5 1.7 %pad_maximum_fusion.7 = (f32[90,1,130]{2,1,0:T(1,128)S(1)}, f32[90,1,130]{2,1,0:T(1,128)S(1)}) fusion(f32[90,32,1]{2,1,0:T(8,128)} %copy.16, f32[90,32,128]{2,1,0:T(8,128)S(1)} %copy-done, f32[90,32,1]{2,1,0:T(8,128)S(1)} %copy.15), kind=kLoop, calls=%fused_computation.22 | loop fusion | flops 46800 | bytes 1591200 | tf_op jit(solution)/shard_map/slice | solution.py:22
  17.2 0.1 collective-permute-start.2
  17.3 1.7 %collective-permute-start.3 = (f32[90,1,130]{2,1,0:T(1,128)S(1)}, f32[90,1,130]{2,1,0:T(1,128)S(1)}, u32[]{:S(2)}, u32[]{:S(2)}) collective-permute-start(f32[90,1,130]{2,1,0:T(1,128)S(1)} %get-tuple-element.53), channel_id=1, source_target_pairs={{1,0},{2,1},{3,2},{0,3},{5,4},{6,5},{7,6},{4,7},{9,8},{10,9},{11,1... | collective-permute-start | bytes 140408 | tf_op jit(solution)/shard_map/ppermute | solution.py:24
  19.0 2.2 %collective-permute-done.2 = f32[90,1,130]{2,1,0:T(1,128)S(1)} collective-permute-done((f32[90,1,130]{2,1,0:T(1,128)S(1)}, f32[90,1,130]{2,1,0:T(1,128)S(1)}, u32[]{:S(2)}, u32[]{:S(2)}) %collective-permute-start.2) | collective-permute-done | bytes 46832 | tf_op jit(solution)/shard_map/ppermute | solution.py:21
  21.3 0.1 collective-permute-done.3
  21.4 4.7 %pad_maximum_fusion = f32[90,34,130]{2,1,0:T(8,128)} fusion(f32[90,1,130]{2,1,0:T(1,128)S(1)} %collective-permute-done.3, f32[90,32,1]{2,1,0:T(8,128)} %copy.16, f32[90,32,128]{2,1,0:T(8,128)S(1)} %copy-done, f32[90,32,1]{2,1,0:T(8,128)S(1)} %copy.15, f32[90,1,130]{2,1,0:T(1,128)S(1)} %collective-permute-done.2), kind=kLoop, calls=%fused_computation | loop fusion | flops 1591200 | bytes 3182400 | tf_op jit(solution)/shard_map/concatenate | solution.py:25
  26.1 0.1 broadcast_multiply_fusion.1
  26.2 3.4 %scatter-mul.14 = f32[90,34,130]{2,1,0:T(8,128)} dynamic-update-slice(f32[90,34,130]{2,1,0:T(8,128)} %pad_maximum_fusion, f32[90,1,130]{2,1,0:T(1,128)S(1)} %broadcast_multiply_fusion.1, s32[]{:T(128)} %constant.102.clone.1, s32[]{:T(128)} %constant.102.clone.1, s32[]{:T(128)} %constant.102.clone.1) | dynamic-update-slice | bytes 93604 | tf_op jit(solution)/shard_map/scatter-mul | solution.py:240
  29.6 1.2 %slice_multiply_fusion.1 = f32[90,1,130]{2,1,0:T(1,128)S(1)} fusion(f32[90,34,130]{2,1,0:T(8,128)} %scatter-mul.14, f32[]{:T(128)S(6)} %select_n.10), kind=kLoop, calls=%fused_computation.19 | loop fusion | flops 11700 | bytes 93604 | tf_op jit(solution)/shard_map/mul | solution.py:241
  30.8 3.4 %scatter-mul.15 = f32[90,34,130]{2,1,0:T(8,128)} dynamic-update-slice(f32[90,34,130]{2,1,0:T(8,128)} %scatter-mul.14, f32[90,1,130]{2,1,0:T(1,128)S(1)} %slice_multiply_fusion.1, s32[]{:T(128)} %constant.102.clone.1, s32[]{:T(128)} %constant.106.clone.1, s32[]{:T(128)} %constant.102.clone.1) | dynamic-update-slice | bytes 93604 | tf_op jit(solution)/shard_map/scatter-mul | solution.py:241
  34.2 0.0 copy-done.14
  34.2 5.8 %fusion.6 = f32[90,32,128]{2,1,0:T(8,128)S(1)} fusion(f32[90,32,128]{2,1,0:T(8,128)S(1)} %copy-done, f32[90,34,130]{2,1,0:T(8,128)} %scatter-mul.15, f32[32,128]{1,0:T(8,128)S(1)} %copy-done.14), kind=kLoop, calls=%fused_computation.12 | loop fusion | flops 2580480 | bytes 8863744 | tf_op jit(solution)/shard_map/add | solution.py:245
  40.1 0.0 copy-start.9
  40.1 2.2 %fusion.7 = (f32[90,32,1]{2,1,0:T(8,128)}, f32[90,32,1]{2,1,0:T(8,128)}) fusion(f32[90,32,128]{2,1,0:T(8,128)S(1)} %fusion.6), kind=kLoop, calls=%fused_computation.25 | loop fusion | bytes 46080 | tf_op jit(solution)/shard_map/slice | solution.py:22
  42.3 2.2 %copy.17 = f32[90,32,1]{0,1,2:T(8,128)S(1)} copy(f32[90,32,1]{2,1,0:T(8,128)} %get-tuple-element.54) | data formatting | bytes 23040 | tf_op jit(solution)/shard_map/slice | solution.py:22
  44.5 0.8 collective-permute-start.4
  45.3 2.2 %copy.18 = f32[90,32,1]{0,1,2:T(8,128)S(1)} copy(f32[90,32,1]{2,1,0:T(8,128)} %get-tuple-element.55) | data formatting | bytes 23040 | tf_op jit(solution)/shard_map/slice | solution.py:24
  47.5 4.1 %collective-permute-start.5 = (f32[90,32,1]{0,1,2:T(8,128)S(1)}, f32[90,32,1]{0,1,2:T(8,128)S(1)}, u32[]{:S(2)}, u32[]{:S(2)}) collective-permute-start(f32[90,32,1]{0,1,2:T(8,128)S(1)} %copy.18), channel_id=1, source_target_pairs={{4,0},{8,4},{12,8},{16,12},{20,16},{24,20},{28,24},{0,28},{5,1},{9... | collective-permute-start | bytes 34568 | tf_op jit(solution)/shard_map/ppermute | solution.py:24
  51.6 0.0 collective-permute-done.4
  51.6 2.3 %copy.19 = f32[90,32,1]{2,1,0:T(8,128)} copy(f32[90,32,1]{0,1,2:T(8,128)S(1)} %collective-permute-done.4) | data formatting | bytes 23040 | tf_op jit(solution)/shard_map/ppermute | solution.py:21
  53.9 0.0 collective-permute-done.5
  53.9 2.3 %copy.20 = f32[90,32,1]{2,1,0:T(8,128)} copy(f32[90,32,1]{0,1,2:T(8,128)S(1)} %collective-permute-done.5) | data formatting | bytes 23040 | tf_op jit(solution)/shard_map/ppermute | solution.py:24
  56.2 0.0 copy-done.9
  56.2 0.0 copy-start.4
  56.2 0.0 copy-start.5
  56.3 0.0 copy-start.6
  56.3 0.0 copy-start.7
  56.3 0.0 copy-start.8
  56.3 2.1 %pad_maximum_fusion.4 = (f32[90,1,130]{2,1,0:T(1,128)S(1)}, f32[90,1,130]{2,1,0:T(1,128)S(1)}) fusion(f32[90,32,1]{2,1,0:T(8,128)} %copy.20, f32[90,32,128]{2,1,0:T(8,128)S(1)} %fusion.6, f32[90,32,1]{2,1,0:T(8,128)} %copy.19), kind=kLoop, calls=%fused_computation.18 | loop fusion | flops 46800 | bytes 1591200 | tf_op jit(solution)/shard_map/slice | solution.py:22
  58.4 1.1 %collective-permute-start.6 = (f32[90,1,130]{2,1,0:T(1,128)S(1)}, f32[90,1,130]{2,1,0:T(1,128)S(1)}, u32[]{:S(2)}, u32[]{:S(2)}) collective-permute-start(f32[90,1,130]{2,1,0:T(1,128)S(1)} %get-tuple-element.50), channel_id=1, source_target_pairs={{0,1},{1,2},{2,3},{3,0},{4,5},{5,6},{6,7},{7,4},{8,9},{9,10},{10,1... | collective-permute-start | bytes 140408 | tf_op jit(solution)/shard_map/ppermute | solution.py:21
  59.5 0.0 copy-done.1
  59.5 0.0 copy-done.2
  59.5 0.0 copy-done.3
  59.5 0.0 copy-done.4
  59.5 0.0 copy-done.5
  59.5 0.0 copy-done.6
  59.5 0.0 copy-done.7
  59.6 0.0 copy-done.8
  59.6 0.0 copy-start.10
  59.6 0.0 copy-start.13
  59.6 20.9 %shard_map.122 = f32[90,32,128]{2,1,0:T(8,128)S(1)} custom-call(f32[90,32,128]{2,1,0:T(8,128)S(1)} %copy-done, f32[90,32,128]{2,1,0:T(8,128)S(1)} %copy-done.1, f32[32,128]{1,0:T(8,128)S(1)} %copy-done.4, s32[32]{0:T(128)S(1)} %bitcast.6, f32[181,512]{1,0:T(8,128)S(1)} %bitcast.4, f32[1,512]{1,0:T(1,128)S(1)} %bitcast.5, f32[2,512,512]{2,1,0:T(8,128)} %wm.1, ...), custom_call_target="tpu_custom_call" | custom-call | tf_op jit(solution)/shard_map/pallas_call | solution.py:186
  80.5 0.1 collective-permute-start.7
  80.6 0.0 collective-permute-done.6
  80.6 0.1 broadcast_multiply_fusion
  80.7 2.1 %collective-permute-done.7 = f32[90,1,130]{2,1,0:T(1,128)S(1)} collective-permute-done((f32[90,1,130]{2,1,0:T(1,128)S(1)}, f32[90,1,130]{2,1,0:T(1,128)S(1)}, u32[]{:S(2)}, u32[]{:S(2)}) %collective-permute-start.7) | collective-permute-done | bytes 46832 | tf_op jit(solution)/shard_map/ppermute | solution.py:24
  82.8 0.0 copy-done.10
  82.8 0.0 copy-done.13
  82.8 3.4 %pad_maximum_fusion.1 = f32[90,34,130]{2,1,0:T(8,128)} fusion(f32[90,1,130]{2,1,0:T(1,128)S(1)} %collective-permute-done.7, f32[90,32,1]{2,1,0:T(8,128)S(1)} %copy-done.13, f32[90,32,128]{2,1,0:T(8,128)S(1)} %copy-done.10, f32[90,32,1]{2,1,0:T(8,128)S(1)} %copy-done.12, f32[90,1,130]{2,1,0:T(1,128)S(1)} %collective-permute-done.6), kind=kLoop, calls=%fused_computation.1 | loop fusion | flops 1591200 | bytes 3182400 | tf_op jit(solution)/shard_map/concatenate | solution.py:25
  86.2 3.4 %scatter-mul.16 = f32[90,34,130]{2,1,0:T(8,128)} dynamic-update-slice(f32[90,34,130]{2,1,0:T(8,128)} %pad_maximum_fusion.1, f32[90,1,130]{2,1,0:T(1,128)S(1)} %broadcast_multiply_fusion, s32[]{:T(128)} %constant.102.clone.1, s32[]{:T(128)} %constant.102.clone.1, s32[]{:T(128)} %constant.102.clone.1) | dynamic-update-slice | bytes 93604 | tf_op jit(solution)/shard_map/scatter-mul | solution.py:240
  89.6 1.2 %slice_multiply_fusion = f32[90,1,130]{2,1,0:T(1,128)S(1)} fusion(f32[90,34,130]{2,1,0:T(8,128)} %scatter-mul.16, f32[]{:T(128)S(6)} %select_n.10), kind=kLoop, calls=%fused_computation.15 | loop fusion | flops 11700 | bytes 93604 | tf_op jit(solution)/shard_map/mul | solution.py:241
  90.8 3.4 %scatter-mul.19 = f32[90,34,130]{2,1,0:T(8,128)} dynamic-update-slice(f32[90,34,130]{2,1,0:T(8,128)} %scatter-mul.16, f32[90,1,130]{2,1,0:T(1,128)S(1)} %slice_multiply_fusion, s32[]{:T(128)} %constant.102.clone.1, s32[]{:T(128)} %constant.106.clone.1, s32[]{:T(128)} %constant.102.clone.1) | dynamic-update-slice | bytes 93604 | tf_op jit(solution)/shard_map/scatter-mul | solution.py:241
  94.2 0.0 copy-done.11
  94.2 6.9 %fusion.3 = f32[90,32,128]{2,1,0:T(8,128)} fusion(f32[90,32,128]{2,1,0:T(8,128)S(1)} %shard_map.122, f32[90,32,128]{2,1,0:T(8,128)S(1)} %copy-done.11, f32[90,34,130]{2,1,0:T(8,128)} %scatter-mul.19, f32[32,128]{1,0:T(8,128)S(1)} %copy-done.14), kind=kLoop, calls=%fused_computation.6 | loop fusion | flops 2949120 | bytes 10338304 | tf_op jit(solution)/shard_map/add | solution.py:260
  101.1 1.1 %copy.28 = f32[90,32,128]{2,1,0:T(8,128)} copy(f32[90,32,128]{2,1,0:T(8,128)S(1)} %shard_map.122) | data formatting | bytes 2949120
  (8 shorter events, 0.0 us)
Async XLA Ops:
  4.0 7.8 %collective-permute-start = (f32[90,32,1]{0,1,2:T(8,128)S(1)}, f32[90,32,1]{0,1,2:T(8,128)S(1)}, u32[]{:S(2)}, u32[]{:S(2)}) collective-permute-start(f32[90,32,1]{0,1,2:T(8,128)S(1)} %copy.21), channel_id=1, source_target_pairs={{0,4},{4,8},{8,12},{12,16},{16,20},{20,24},{24,28},{28,0},{1,5},{5... | collective-permute-start | bytes 34568 | tf_op jit(solution)/shard_map/ppermute | solution.py:21
  7.9 7.6 %copy-start = (f32[90,32,128]{2,1,0:T(8,128)S(1)}, f32[90,32,128]{2,1,0:T(8,128)}, u32[]{:S(2)}) copy-start(f32[90,32,128]{2,1,0:T(8,128)} %temp.1) | copy-start | bytes 4423684
  7.9 5.3 %collective-permute-start.1 = (f32[90,32,1]{0,1,2:T(8,128)S(1)}, f32[90,32,1]{0,1,2:T(8,128)S(1)}, u32[]{:S(2)}, u32[]{:S(2)}) collective-permute-start(f32[90,32,1]{0,1,2:T(8,128)S(1)} %copy.22), channel_id=1, source_target_pairs={{4,0},{8,4},{12,8},{16,12},{20,16},{24,20},{28,24},{0,28},{5,1},{9... | collective-permute-start | bytes 34568 | tf_op jit(solution)/shard_map/ppermute | solution.py:24
  17.2 4.0 %collective-permute-start.2 = (f32[90,1,130]{2,1,0:T(1,128)S(1)}, f32[90,1,130]{2,1,0:T(1,128)S(1)}, u32[]{:S(2)}, u32[]{:S(2)}) collective-permute-start(f32[90,1,130]{2,1,0:T(1,128)S(1)} %get-tuple-element.52), channel_id=1, source_target_pairs={{0,1},{1,2},{2,3},{3,0},{4,5},{5,6},{6,7},{7,4},{8,9},{9,10},{10,1... | collective-permute-start | bytes 140408 | tf_op jit(solution)/shard_map/ppermute | solution.py:21
  17.3 4.1 %collective-permute-start.3 = (f32[90,1,130]{2,1,0:T(1,128)S(1)}, f32[90,1,130]{2,1,0:T(1,128)S(1)}, u32[]{:S(2)}, u32[]{:S(2)}) collective-permute-start(f32[90,1,130]{2,1,0:T(1,128)S(1)} %get-tuple-element.53), channel_id=1, source_target_pairs={{1,0},{2,1},{3,2},{0,3},{5,4},{6,5},{7,6},{4,7},{9,8},{10,9},{11,1... | collective-permute-start | bytes 140408 | tf_op jit(solution)/shard_map/ppermute | solution.py:24
  19.0 15.2 %copy-start.14 = (f32[32,128]{1,0:T(8,128)S(1)}, f32[32,128]{1,0:T(8,128)}, u32[]{:S(2)}) copy-start(f32[32,128]{1,0:T(8,128)} %param.23) | copy-start | bytes 49156
  40.1 16.1 %copy-start.9 = (f32[90,32,128]{2,1,0:T(8,128)}, f32[90,32,128]{2,1,0:T(8,128)S(1)}, u32[]{:S(2)}) copy-start(f32[90,32,128]{2,1,0:T(8,128)S(1)} %fusion.6) | copy-start | bytes 4423684
  44.5 7.1 %collective-permute-start.4 = (f32[90,32,1]{0,1,2:T(8,128)S(1)}, f32[90,32,1]{0,1,2:T(8,128)S(1)}, u32[]{:S(2)}, u32[]{:S(2)}) collective-permute-start(f32[90,32,1]{0,1,2:T(8,128)S(1)} %copy.17), channel_id=1, source_target_pairs={{0,4},{4,8},{8,12},{12,16},{16,20},{20,24},{24,28},{28,0},{1,5},{5... | collective-permute-start | bytes 34568 | tf_op jit(solution)/shard_map/ppermute | solution.py:21
  47.5 6.4 %collective-permute-start.5 = (f32[90,32,1]{0,1,2:T(8,128)S(1)}, f32[90,32,1]{0,1,2:T(8,128)S(1)}, u32[]{:S(2)}, u32[]{:S(2)}) collective-permute-start(f32[90,32,1]{0,1,2:T(8,128)S(1)} %copy.18), channel_id=1, source_target_pairs={{4,0},{8,4},{12,8},{16,12},{20,16},{24,20},{28,24},{0,28},{5,1},{9... | collective-permute-start | bytes 34568 | tf_op jit(solution)/shard_map/ppermute | solution.py:24
  56.2 3.3 %copy-start.1 = (f32[90,32,128]{2,1,0:T(8,128)S(1)}, f32[90,32,128]{2,1,0:T(8,128)}, u32[]{:S(2)}) copy-start(f32[90,32,128]{2,1,0:T(8,128)} %moist.1) | copy-start | bytes 4423684
  56.2 3.3 %copy-start.2 = (f32[512,181]{0,1:T(8,128)S(1)}, f32[512,181]{0,1:T(8,128)}, u32[]{:S(2)}) copy-start(f32[512,181]{0,1:T(8,128)} %param.24) | copy-start | bytes 1112068
  56.2 3.3 %copy-start.3 = (f32[90,512]{1,0:T(8,128)S(1)}, f32[90,512]{1,0:T(8,128)}, u32[]{:S(2)}) copy-start(f32[90,512]{1,0:T(8,128)} %wf.1) | copy-start | bytes 552964
  56.2 3.3 %copy-start.4 = (f32[32,128]{1,0:T(8,128)S(1)}, f32[32,128]{1,0:T(8,128)}, u32[]{:S(2)}) copy-start(f32[32,128]{1,0:T(8,128)} %mu.1) | copy-start | bytes 49156
  56.2 3.3 %copy-start.5 = (f32[2,512]{1,0:T(2,128)S(1)}, f32[2,512]{1,0:T(2,128)}, u32[]{:S(2)}) copy-start(f32[2,512]{1,0:T(2,128)} %bm.1) | copy-start | bytes 12292
  56.3 3.3 %copy-start.6 = (f32[512]{0:T(512)S(1)}, f32[512]{0:T(512)}, u32[]{:S(2)}) copy-start(f32[512]{0:T(512)} %param.25) | copy-start | bytes 6148
  56.3 3.3 %copy-start.7 = (s32[32,1]{0,1:T(1,128)S(1)}, s32[32,1]{0,1:T(1,128)}, u32[]{:S(2)}) copy-start(s32[32,1]{0,1:T(1,128)} %param.22) | copy-start | bytes 388
  56.3 3.3 %copy-start.8 = (f32[90]{0:T(128)S(1)}, f32[90]{0:T(128)}, u32[]{:S(2)}) copy-start(f32[90]{0:T(128)} %param.29) | copy-start | bytes 1084
  58.4 22.2 %collective-permute-start.6 = (f32[90,1,130]{2,1,0:T(1,128)S(1)}, f32[90,1,130]{2,1,0:T(1,128)S(1)}, u32[]{:S(2)}, u32[]{:S(2)}) collective-permute-start(f32[90,1,130]{2,1,0:T(1,128)S(1)} %get-tuple-element.50), channel_id=1, source_target_pairs={{0,1},{1,2},{2,3},{3,0},{4,5},{5,6},{6,7},{7,4},{8,9},{9,10},{10,1... | collective-permute-start | bytes 140408 | tf_op jit(solution)/shard_map/ppermute | solution.py:21
  59.6 23.2 %copy-start.10 = (f32[90,32,128]{2,1,0:T(8,128)S(1)}, f32[90,32,128]{2,1,0:T(8,128)}, u32[]{:S(2)}) copy-start(f32[90,32,128]{2,1,0:T(8,128)} %copy-done.9) | copy-start | bytes 4423684
  59.6 23.2 %copy-start.12 = (f32[90,32,1]{2,1,0:T(8,128)S(1)}, f32[90,32,1]{2,1,0:T(8,128)}, u32[]{:S(2)}) copy-start(f32[90,32,1]{2,1,0:T(8,128)} %copy.19) | copy-start | bytes 34564
  59.6 23.2 %copy-start.13 = (f32[90,32,1]{2,1,0:T(8,128)S(1)}, f32[90,32,1]{2,1,0:T(8,128)}, u32[]{:S(2)}) copy-start(f32[90,32,1]{2,1,0:T(8,128)} %copy.20) | copy-start | bytes 34564
  80.5 2.3 %collective-permute-start.7 = (f32[90,1,130]{2,1,0:T(1,128)S(1)}, f32[90,1,130]{2,1,0:T(1,128)S(1)}, u32[]{:S(2)}, u32[]{:S(2)}) collective-permute-start(f32[90,1,130]{2,1,0:T(1,128)S(1)} %get-tuple-element.51), channel_id=1, source_target_pairs={{1,0},{2,1},{3,2},{0,3},{5,4},{6,5},{7,6},{4,7},{9,8},{10,9},{11,1... | collective-permute-start | bytes 140408 | tf_op jit(solution)/shard_map/ppermute | solution.py:24
  82.8 11.4 %copy-start.11 = (f32[90,32,128]{2,1,0:T(8,128)S(1)}, f32[90,32,128]{2,1,0:T(8,128)}, u32[]{:S(2)}) copy-start(f32[90,32,128]{2,1,0:T(8,128)} %copy-done.9) | copy-start | bytes 4423684

commit v2 on v1

v2 whole, which is shorter than its diff:
```python
import jax
import jax.numpy as jnp
from jax import lax
from jax.experimental import pallas as pl
from jax.experimental.pallas import tpu as pltpu
from jax.sharding import PartitionSpec as P

MESH = pl.DeviceIdType.MESH
GROUP = 4
EDGE = 4
PAD = 8


def up8(n):
    return (n + 7) // 8 * 8


def split(x):
    hi = x.astype(jnp.bfloat16)
    lo = (x - hi.astype(jnp.float32)).astype(jnp.bfloat16)
    return hi, lo


def dot(a, b):
    return jnp.dot(a, b, preferred_element_type=jnp.float32)


def dot3(w_hi, w_lo, x):
    hi, lo = split(x)
    return dot(w_hi, hi) + dot(w_hi, lo) + dot(w_lo, hi)


def gate(h):
    return h + h * jnp.tanh(h)


def roll(x, shift, axis):
    return pltpu.roll(x, shift % x.shape[axis], axis)


def kernel(
    temp, moist, mu, lit, spread, w0t, b0, wm, bm, wf, bf,
    heat, nxt,
    temp_v, moist_v, mu_v, spread_v, temp_r, moist_r, mu_r,
    w0_hi, w0_lo, wm_hi, wm_lo, wf_hi, wf_lo, b0_c, bm_c, bf_c,
    xs, res, res_r,
    temp_t, temp_b, spread_t, spread_b,
    pack, left_m, left_t, left_b, right_m, right_t, right_b,
    edge_0, edge_1,
    in_sem, send_sem, recv_sem, out_send, out_recv, halo_send, halo_recv,
):
    levels, rows, lanes = temp.shape
    half = rows // 2
    hid = wm.shape[1]
    depth = wm.shape[0]
    lp = up8(levels)
    tiles = pack.shape[0] - 1
    slots = lanes // EDGE
    n_lat = lax.axis_size("lat")
    n_lon = lax.axis_size("lon")
    lat = lax.axis_index("lat")
    lon = lax.axis_index("lon")
    parity = lax.rem(lat, 2)
    partner = lat + 1 - 2 * parity
    mine = pl.multiple_of(parity * half, half)
    theirs = pl.multiple_of(half - parity * half, half)
    left = lax.rem(lon + n_lon - 1, n_lon)
    right = lax.rem(lon + 1, n_lon)
    has_up = lat > 0
    has_down = lat < n_lat - 1
    up = jnp.maximum(lat - 1, 0)
    down = jnp.minimum(lat + 1, n_lat - 1)

    own = [
        pltpu.make_async_copy(src, dst, in_sem.at[i])
        for i, (src, dst) in enumerate((
            (temp, temp_v), (moist, moist_v), (mu, mu_v), (spread, spread_v)))
    ]
    for copy in own:
        copy.start()

    def at(lat_to, lon_to):
        return {"lat": lat_to, "lon": lon_to}

    barrier = pltpu.get_barrier_semaphore()

    def hello(lat_to, lon_to):
        pl.semaphore_signal(barrier, inc=1, device_id=at(lat_to, lon_to), device_id_type=MESH)

    hello(lat, left)
    hello(lat, right)

    @pl.when(has_up)
    def _():
        for to in (left, lon, right):
            hello(up, to)

    @pl.when(has_down)
    def _():
        for to in (left, lon, right):
            hello(down, to)

    pl.semaphore_wait(
        barrier, 2 + 3 * has_up.astype(jnp.int32) + 3 * has_down.astype(jnp.int32))

    out = [
        pltpu.make_async_remote_copy(
            src_ref=src, dst_ref=dst, send_sem=send_sem.at[i], recv_sem=recv_sem.at[i],
            device_id=at(partner, lon), device_id_type=MESH)
        for i, (src, dst) in enumerate((
            (mu.at[pl.ds(theirs, half), :], mu_r),
            (temp.at[:, pl.ds(theirs, half), :], temp_r),
            (moist.at[:, pl.ds(theirs, half), :], moist_r),
        ))
    ]
    for copy in out:
        copy.start()

    first, last = pl.ds(0, PAD), pl.ds(rows - PAD, PAD)

    def halo(i, src, dst, lat_to, lon_to):
        return pltpu.make_async_remote_copy(
            src_ref=src, dst_ref=dst, send_sem=halo_send.at[i], recv_sem=halo_recv.at[i],
            device_id=at(lat_to, lon_to), device_id_type=MESH)

    beside = [
        halo(0, pack, right_m, lat, left),
        halo(1, pack, left_m, lat, right),
    ]
    to_up = [
        halo(2, spread.at[first, :], spread_b, up, lon),
        halo(3, temp.at[:, first, :], temp_b, up, lon),
        halo(4, pack.at[:, first, :], right_b, up, left),
        halo(5, pack.at[:, first, :], left_b, up, right),
    ]
    to_down = [
        halo(6, spread.at[last, :], spread_t, down, lon),
        halo(7, temp.at[:, last, :], temp_t, down, lon),
        halo(8, pack.at[:, last, :], right_t, down, left),
        halo(9, pack.at[:, last, :], left_t, down, right),
    ]

    for copy in (own[0], own[3], own[2]):
        copy.wait()
    lane = lax.broadcasted_iota(jnp.int32, (rows, lanes), 1)
    for t in range(tiles):
        count = min(slots, levels - t * slots)
        acc = jnp.zeros((rows, lanes), jnp.float32)
        for m in range(count):
            moved = roll(temp_v[t * slots + m], EDGE * m + 2, 1)
            acc = jnp.where(lane // EDGE == m, moved, acc)
        pack[t] = acc
    acc = jnp.where(lane < EDGE, roll(spread_v[...], 2, 1), 0.0)
    step = EDGE
    while step < lanes:
        acc = acc + roll(acc, step, 1)
        step *= 2
    pack[tiles] = acc

    for copy in beside:
        copy.start()

    @pl.when(has_up)
    def _():
        for copy in to_up:
            copy.start()

    @pl.when(has_down)
    def _():
        for copy in to_down:
            copy.start()

    @pl.when(jnp.logical_not(has_up))
    def _():
        for ref in (temp_t, spread_t, left_t, right_t):
            ref[...] = jnp.zeros_like(ref)

    @pl.when(jnp.logical_not(has_down))
    def _():
        for ref in (temp_b, spread_b, left_b, right_b):
            ref[...] = jnp.zeros_like(ref)

    xs[...] = jnp.zeros_like(xs)
    xs[0:levels, 0:hid] = w0t[0:levels, :] * 0.5
    xs[lp:lp + levels, 0:hid] = w0t[levels:2 * levels, :] * 0.5
    xs[2 * lp:2 * lp + 1, 0:hid] = w0t[2 * levels:2 * levels + 1, :] * 0.5
    w0_hi[...], w0_lo[...] = split(xs[:, 0:hid].T)
    for k in range(depth):
        wm_hi[k], wm_lo[k] = split(wm[k] * 0.5)
    wf_hi[...], wf_lo[...] = split(wf[...])

    def column(row):
        return jnp.broadcast_to(row, (lanes, row.shape[1])).T

    b0_c[...] = column(b0[...] * 0.5)
    for k in range(depth):
        bm_c[k] = column(bm[k:k + 1, :] * 0.5)
    bf_c[...] = column(bf[...])
    xs[...] = jnp.zeros_like(xs)

    own[1].wait()
    for copy in out:
        copy.wait()

    temp_f = temp_v.reshape(levels * rows, lanes)
    moist_f = moist_v.reshape(levels * rows, lanes)
    temp_rf = temp_r.reshape(levels * half, lanes)
    moist_rf = moist_r.reshape(levels * half, lanes)

    def wide(c):
        return jnp.concatenate([c] * GROUP, axis=1)

    def send(g):
        rows_g = pl.ds(g * GROUP, GROUP)
        return pltpu.make_async_remote_copy(
            src_ref=res.at[rows_g], dst_ref=res_r.at[rows_g],
            send_sem=out_send.at[g], recv_sem=out_recv.at[g],
            device_id=at(partner, lon), device_id_type=MESH)

    def network(g, carry):
        for j in range(GROUP):
            i = g * GROUP + j
            r = mine + i
            on = lit[r].astype(jnp.float32)
            off = 1.0 - on
            cols = slice(j * lanes, (j + 1) * lanes)
            xs[0:levels, cols] = (
                temp_f[pl.ds(r, levels, stride=rows), :] * on
                + temp_rf[pl.ds(i, levels, stride=half), :] * off)
            xs[lp:lp + levels, cols] = (
                moist_f[pl.ds(r, levels, stride=rows), :] * on
                + moist_rf[pl.ds(i, levels, stride=half), :] * off)
            xs[2 * lp:2 * lp + 1, cols] = (
                mu_v[pl.ds(r, 1), :] * on + mu_r[pl.ds(i, 1), :] * off)
        h = gate(dot3(w0_hi[...], w0_lo[...], xs[...]) + wide(b0_c[...]))
        for k in range(depth):
            h = gate(dot3(wm_hi[k], wm_lo[k], h) + wide(bm_c[k]))
        y = dot3(wf_hi[...], wf_lo[...], h) + wide(bf_c[...])
        y = y * xs[2 * lp:2 * lp + 1, :]
        for j in range(GROUP):
            res[g * GROUP + j] = y[:, j * lanes:(j + 1) * lanes]
        send(g).start()
        return carry

    lax.fori_loop(0, half // GROUP, network, 0)

    for copy in beside:
        copy.wait()

    @pl.when(has_up)
    def _():
        for copy in to_up:
            copy.wait_send()
        for copy in to_down:
            copy.wait_recv()

    @pl.when(has_down)
    def _():
        for copy in to_down:
            copy.wait_send()
        for copy in to_up:
            copy.wait_recv()

    tall = rows + 2 * PAD

    def stack(top, middle, bottom):
        return jnp.concatenate([top, middle, bottom], axis=0)

    def advance(x, f, west, east):
        beside = roll(x, 1, 0) + roll(x, tall - 1, 0) + west + east
        return x + f * (beside - 4.0 * x)

    slot = lax.broadcasted_iota(jnp.int32, (tall, lanes), 1)
    place = lax.rem(slot, EDGE)
    zero8 = jnp.zeros((PAD, lanes), jnp.float32)

    def gather(t):
        lhs = stack(left_t[t], left_m[t], left_b[t])
        rhs = stack(right_t[t], right_m[t], right_b[t])
        here = stack(zero8, pack[t], zero8)
        return (jnp.where(place < 2, lhs, here), jnp.where(place < 2, here, rhs))

    f_west, f_east = gather(tiles)
    for t in range(tiles):
        west, east = gather(t)
        edge_0[t] = jnp.where(place == 1, roll(east, lanes - 1, 1), roll(west, 1, 1))
        west = advance(west, f_west, roll(west, 1, 1), roll(west, lanes - 1, 1))
        east = advance(east, f_east, roll(east, 1, 1), roll(east, lanes - 1, 1))
        edge_1[t] = jnp.where(place == 1, roll(east, lanes - 1, 1), roll(west, 1, 1))

    f_all = stack(spread_t[...], spread_v[...], spread_b[...])
    for k in range(levels):
        t, m = divmod(k, slots)
        turn = lanes - 2 - EDGE * m
        x = stack(temp_t[k], temp_v[k], temp_b[k])
        for edge in (edge_0, edge_1):
            rim = roll(edge[t], turn, 1)
            west = jnp.where(slot == 0, rim, roll(x, 1, 1))
            east = jnp.where(slot == lanes - 1, rim, roll(x, lanes - 1, 1))
            x = advance(x, f_all, west, east)
        nxt[k] = x[PAD:PAD + rows]

    heat_f = heat.reshape(levels * rows, lanes)
    nxt_f = nxt.reshape(levels * rows, lanes)

    def place_row(r, value):
        there = pl.ds(r, levels, stride=rows)
        value = value * lit[r].astype(jnp.float32)
        heat_f[there, :] = value
        nxt_f[there, :] = nxt_f[there, :] + value

    for i in range(half):
        place_row(mine + i, res[i])
    for g in range(half // GROUP):
        send(g).wait()
    for i in range(half):
        place_row(theirs + i, res_r[i])


def run(temp, moist, mu, lit, spread, w0, b0, wm, bm, wf, bf):
    levels, rows, lanes = temp.shape
    half = rows // 2
    hid = wm.shape[1]
    depth = wm.shape[0]
    lp = up8(levels)
    kp = (2 * lp + 256) // 256 * 256
    tall = rows + 2 * PAD
    tiles = (levels * EDGE + lanes - 1) // lanes
    f32, bf16 = jnp.float32, jnp.bfloat16
    vmem = pl.BlockSpec(memory_space=pltpu.VMEM)
    hbm = pl.BlockSpec(memory_space=pltpu.HBM)
    smem = pl.BlockSpec(memory_space=pltpu.SMEM)
    groups = half // GROUP
    dma = pltpu.SemaphoreType.DMA

    def buf(*shape, dtype=f32):
        return pltpu.VMEM(shape, dtype)

    return pl.pallas_call(
        kernel,
        out_shape=(jax.ShapeDtypeStruct(temp.shape, f32),) * 2,
        in_specs=[hbm, hbm, hbm, smem, hbm] + [vmem] * 6,
        out_specs=(vmem, vmem),
        scratch_shapes=[
            buf(levels, rows, lanes), buf(levels, rows, lanes), buf(rows, lanes), buf(rows, lanes),
            buf(levels, half, lanes), buf(levels, half, lanes), buf(half, lanes),
            buf(hid, kp, dtype=bf16), buf(hid, kp, dtype=bf16),
            buf(depth, hid, hid, dtype=bf16), buf(depth, hid, hid, dtype=bf16),
            buf(levels, hid, dtype=bf16), buf(levels, hid, dtype=bf16),
            buf(hid, lanes), buf(depth, hid, lanes), buf(levels, lanes),
            buf(kp, max(hid, GROUP * lanes)), buf(half, levels, lanes), buf(half, levels, lanes),
            buf(levels, PAD, lanes), buf(levels, PAD, lanes), buf(PAD, lanes), buf(PAD, lanes),
            buf(tiles + 1, rows, lanes),
            buf(tiles + 1, rows, lanes), buf(tiles + 1, PAD, lanes), buf(tiles + 1, PAD, lanes),
            buf(tiles + 1, rows, lanes), buf(tiles + 1, PAD, lanes), buf(tiles + 1, PAD, lanes),
            buf(tiles, tall, lanes), buf(tiles, tall, lanes),
            dma((4,)), dma((3,)), dma((3,)), dma((groups,)), dma((groups,)),
            dma((10,)), dma((10,)),
        ],
        compiler_params=pltpu.CompilerParams(
            collective_id=0, has_side_effects=True, vmem_limit_bytes=48 << 20),
    )(temp, moist, mu, lit, spread, w0.T, b0[None, :], wm, bm, wf, bf[None, :])


def on_device(
    thermal_departure,
    moisture_profile,
    solar_elevation_factor,
    daylight_groups,
    spreading_factor,
    entry_layer_matrix,
    entry_layer_offset,
    inner_layer_matrices,
    inner_layer_offsets,
    final_layer_matrix,
    final_layer_offset,
):
    return tuple(run(
        thermal_departure,
        moisture_profile,
        solar_elevation_factor,
        daylight_groups[:, 0],
        spreading_factor,
        entry_layer_matrix,
        entry_layer_offset,
        inner_layer_matrices,
        inner_layer_offsets,
        final_layer_matrix,
        final_layer_offset,
    ))


def solution(mesh):
    in_specs = (
        P(None, "lat", "lon"),
        P(None, "lat", "lon"),
        P("lat", "lon"),
        P("lat", "lon"),
        P("lat", "lon"),
        P(),
        P(),
        P(),
        P(),
        P(),
        P(),
    )
    out_specs = (P(None, "lat", "lon"), P(None, "lat", "lon"))
    return jax.shard_map(
        on_device, mesh=mesh, in_specs=in_specs, out_specs=out_specs, check_vma=False
    )
```

time: 104 us -> 45.9 us (0.44); the launches traced: 102 us -> 45.5 us
  other arithmetic: 27.3 us -> 0 us
  local copies, waits for them, and re-layouts: 34.1 us -> 9.61 us
  Pallas kernels: 20.9 us -> 35.2 us
  starting transfers between devices: 14 us -> 0 us
  waiting for transfers between devices: 5.25 us -> 0 us
    pallas_call x1, Pallas kernels: 20.9 us -> 35.2 us  [run(): pl.pallas_call(kernel, out_shape=(jax.ShapeDtypeStruct(temp.shape, f32),)...]
    ppermute x8 -> x0, starting transfers between devices: 14 us -> none  [the longest x4 8.99 us: padded_2(): lax.ppermute(lax.slice_in_dim(block, 0, width, axis=dim), axis, backward)]
    another operation x4 -> x0, local copies, waits for them, and re-layouts: 13.7 us -> none  [the longest x2 6.86 us: on_device(): padded = padded.at[:, -1, :].multiply(jnp.where(lat_last, 0.0, 1.0))]
    add x2 -> x0, other arithmetic: 12.8 us -> none  [the longest x1 6.95 us: on_device(): return (heating, atmosphere_snapshot + heating)]
    slice x4 -> x0, local copies, waits for them, and re-layouts: 8.97 us -> none  [the longest x3 6.78 us: padded_2(): lax.slice_in_dim(block, block.shape[dim] - width, None, axis=dim)]
    ppermute x4 -> x0, local copies, waits for them, and re-layouts: 8.27 us -> none  [the longest x2 4.57 us: padded_2(): lax.ppermute(lax.slice_in_dim(block, 0, width, axis=dim), axis, backward)]
    concatenate x2 -> x0, other arithmetic: 8.1 us -> none  [padded_2(): block = jnp.concatenate([low, block, high], axis=dim)]
    unnamed x33 -> x20, local copies, waits for them, and re-layouts: 3.13 us -> 9.61 us
  transfers between devices with their start and end apart: 8 -> 0, of which waited for: 4 -> 0; matrix products, arithmetic and copies ran while one was open for 7% -> 0% of each run, Pallas kernels for 20% -> 0%
where the time goes in v2:
time: 45.9 us; the launch traced here: 45.5 us
  Pallas kernels  35.2 us (77%)
  local copies, waits for them, and re-layouts  9.61 us (21%)
  between operations  0.66 us (1%)
    pallas_call x1, Pallas kernels, run(): pl.pallas_call(kernel, out_shape=(jax.ShapeDtypeStruct(temp.shape, f32),)...  35.2 us
    unnamed x20, local copies, waits for them, and re-layouts  9.61 us

profile of v2, /device:TPU:0, one launch (start us, length us, event | category | flops | bytes accessed | tf_op | source)
XLA Modules:
  0.0 45.5 jit_solution(4347739378916742334)
XLA Ops:
  0.6 0.0 copy-start
  0.6 1.4 %copy-done = f32[90,32,128]{2,1,0:T(8,128)S(1)} copy-done((f32[90,32,128]{2,1,0:T(8,128)S(1)}, f32[90,32,128]{2,1,0:T(8,128)}, u32[]{:S(2)}) %copy-start) | copy-done | bytes 1474584
  2.0 0.0 copy-start.1
  2.0 1.0 %copy-done.1 = f32[512,181]{0,1:T(8,128)S(1)} copy-done((f32[512,181]{0,1:T(8,128)S(1)}, f32[512,181]{0,1:T(8,128)}, u32[]{:S(2)}) %copy-start.1) | copy-done | bytes 370712
  3.0 0.0 copy-start.2
  3.0 0.9 %copy-done.2 = f32[90,512]{1,0:T(8,128)S(1)} copy-done((f32[90,512]{1,0:T(8,128)S(1)}, f32[90,512]{1,0:T(8,128)}, u32[]{:S(2)}) %copy-start.2) | copy-done | bytes 184344
  3.9 0.0 copy-start.3
  3.9 0.7 %copy-done.3 = f32[32,128]{1,0:T(8,128)S(1)} copy-done((f32[32,128]{1,0:T(8,128)S(1)}, f32[32,128]{1,0:T(8,128)}, u32[]{:S(2)}) %copy-start.3) | copy-done | bytes 16408
  4.6 0.0 copy-start.4
  4.6 0.7 %copy-done.4 = f32[32,128]{1,0:T(8,128)S(1)} copy-done((f32[32,128]{1,0:T(8,128)S(1)}, f32[32,128]{1,0:T(8,128)}, u32[]{:S(2)}) %copy-start.4) | copy-done | bytes 16408
  5.4 0.0 copy-start.5
  5.4 0.7 %copy-done.5 = f32[2,512]{1,0:T(2,128)S(1)} copy-done((f32[2,512]{1,0:T(2,128)S(1)}, f32[2,512]{1,0:T(2,128)}, u32[]{:S(2)}) %copy-start.5) | copy-done | bytes 4120
  6.0 0.0 copy-start.6
  6.1 0.7 %copy-done.6 = f32[512]{0:T(512)S(1)} copy-done((f32[512]{0:T(512)S(1)}, f32[512]{0:T(512)}, u32[]{:S(2)}) %copy-start.6) | copy-done | bytes 2072
  6.7 0.0 copy-start.7
  6.7 0.7 %copy-done.7 = s32[32,1]{0,1:T(1,128)S(1)} copy-done((s32[32,1]{0,1:T(1,128)S(1)}, s32[32,1]{0,1:T(1,128)}, u32[]{:S(2)}) %copy-start.7) | copy-done | bytes 152
  7.4 0.0 copy-start.8
  7.4 0.7 %copy-done.8 = f32[90]{0:T(128)S(1)} copy-done((f32[90]{0:T(128)S(1)}, f32[90]{0:T(128)}, u32[]{:S(2)}) %copy-start.8) | copy-done | bytes 384
  8.0 35.2 %shard_map.122 = (f32[90,32,128]{2,1,0:T(8,128)S(1)}, f32[90,32,128]{2,1,0:T(8,128)S(1)}) custom-call(f32[90,32,128]{2,1,0:T(8,128)S(1)} %copy-done, f32[90,32,128]{2,1,0:T(8,128)} %moist.1, f32[32,128]{1,0:T(8,128)S(1)} %copy-done.3, s32[32]{0:T(128)S(1)} %bitcast.6, f32[32,128]{1,0:T(8,128)S(1)} %copy-done.4, f32[181,512]{1,0:T(8,128)S(1)} %bitcast.4, ...), custom_call_target="tpu_custom_call" | custom-call | tf_op jit(solution)/shard_map/pallas_call | solution.py:339
  43.2 1.1 %copy.15 = f32[90,32,128]{2,1,0:T(8,128)} copy(f32[90,32,128]{2,1,0:T(8,128)S(1)} %get-tuple-element.4) | data formatting | bytes 2949120
  44.4 1.1 %copy.16 = f32[90,32,128]{2,1,0:T(8,128)} copy(f32[90,32,128]{2,1,0:T(8,128)S(1)} %get-tuple-element.5) | data formatting | bytes 2949120
Async XLA Ops:
  0.6 1.4 %copy-start = (f32[90,32,128]{2,1,0:T(8,128)S(1)}, f32[90,32,128]{2,1,0:T(8,128)}, u32[]{:S(2)}) copy-start(f32[90,32,128]{2,1,0:T(8,128)} %temp.1) | copy-start | bytes 4423684
  2.0 1.0 %copy-start.1 = (f32[512,181]{0,1:T(8,128)S(1)}, f32[512,181]{0,1:T(8,128)}, u32[]{:S(2)}) copy-start(f32[512,181]{0,1:T(8,128)} %param.16) | copy-start | bytes 1112068
  3.0 0.9 %copy-start.2 = (f32[90,512]{1,0:T(8,128)S(1)}, f32[90,512]{1,0:T(8,128)}, u32[]{:S(2)}) copy-start(f32[90,512]{1,0:T(8,128)} %wf.1) | copy-start | bytes 552964
  3.9 0.7 %copy-start.3 = (f32[32,128]{1,0:T(8,128)S(1)}, f32[32,128]{1,0:T(8,128)}, u32[]{:S(2)}) copy-start(f32[32,128]{1,0:T(8,128)} %mu.1) | copy-start | bytes 49156
  4.6 0.7 %copy-start.4 = (f32[32,128]{1,0:T(8,128)S(1)}, f32[32,128]{1,0:T(8,128)}, u32[]{:S(2)}) copy-start(f32[32,128]{1,0:T(8,128)} %spread.1) | copy-start | bytes 49156
  5.4 0.7 %copy-start.5 = (f32[2,512]{1,0:T(2,128)S(1)}, f32[2,512]{1,0:T(2,128)}, u32[]{:S(2)}) copy-start(f32[2,512]{1,0:T(2,128)} %bm.1) | copy-start | bytes 12292
  6.0 0.7 %copy-start.6 = (f32[512]{0:T(512)S(1)}, f32[512]{0:T(512)}, u32[]{:S(2)}) copy-start(f32[512]{0:T(512)} %param.17) | copy-start | bytes 6148
  6.7 0.7 %copy-start.7 = (s32[32,1]{0,1:T(1,128)S(1)}, s32[32,1]{0,1:T(1,128)}, u32[]{:S(2)}) copy-start(s32[32,1]{0,1:T(1,128)} %param.14) | copy-start | bytes 388
  7.4 0.7 %copy-start.8 = (f32[90]{0:T(128)S(1)}, f32[90]{0:T(128)}, u32[]{:S(2)}) copy-start(f32[90]{0:T(128)} %param.21) | copy-start | bytes 1084

commit v3 on v2

--- a/solution.py
+++ b/solution.py
@@ -8,6 +8,7 @@
 MESH = pl.DeviceIdType.MESH
 GROUP = 4
 EDGE = 4
+CHUNKS = 2
 PAD = 8
 
 
@@ -39,20 +40,22 @@
 
 
 def kernel(
-    temp, moist, mu, lit, spread, w0t, b0, wm, bm, wf, bf,
+    temp, moist, mu, lit_h, spread, w0t_h, b0_h, wm_h, bm_h, wf_h, bf_h,
     heat, nxt,
+    lit, w0t, b0, wm, bm, wf, bf,
     temp_v, moist_v, mu_v, spread_v, temp_r, moist_r, mu_r,
     w0_hi, w0_lo, wm_hi, wm_lo, wf_hi, wf_lo, b0_c, bm_c, bf_c,
     xs, res, res_r,
     temp_t, temp_b, spread_t, spread_b,
     pack, left_m, left_t, left_b, right_m, right_t, right_b,
-    edge_0, edge_1,
+    edge_0, edge_1, f_all,
     in_sem, send_sem, recv_sem, out_send, out_recv, halo_send, halo_recv,
 ):
     levels, rows, lanes = temp.shape
     half = rows // 2
-    hid = wm.shape[1]
-    depth = wm.shape[0]
+    hid = wm_h.shape[1]
+    depth = wm_h.shape[0]
+    groups = half // GROUP
     lp = up8(levels)
     tiles = pack.shape[0] - 1
     slots = lanes // EDGE
@@ -74,11 +77,9 @@
     own = [
         pltpu.make_async_copy(src, dst, in_sem.at[i])
         for i, (src, dst) in enumerate((
-            (temp, temp_v), (moist, moist_v), (mu, mu_v), (spread, spread_v)))
+            (temp, temp_v), (spread, spread_v), (w0t_h, w0t), (wm_h, wm), (wf_h, wf),
+            (b0_h, b0), (bm_h, bm), (bf_h, bf), (mu, mu_v), (lit_h, lit), (moist, moist_v)))
     ]
-    for copy in own:
-        copy.start()
-
     def at(lat_to, lon_to):
         return {"lat": lat_to, "lon": lon_to}
 
@@ -100,20 +101,7 @@
         for to in (left, lon, right):
             hello(down, to)
 
-    pl.semaphore_wait(
-        barrier, 2 + 3 * has_up.astype(jnp.int32) + 3 * has_down.astype(jnp.int32))
-
-    out = [
-        pltpu.make_async_remote_copy(
-            src_ref=src, dst_ref=dst, send_sem=send_sem.at[i], recv_sem=recv_sem.at[i],
-            device_id=at(partner, lon), device_id_type=MESH)
-        for i, (src, dst) in enumerate((
-            (mu.at[pl.ds(theirs, half), :], mu_r),
-            (temp.at[:, pl.ds(theirs, half), :], temp_r),
-            (moist.at[:, pl.ds(theirs, half), :], moist_r),
-        ))
-    ]
-    for copy in out:
+    for copy in own:
         copy.start()
 
     first, last = pl.ds(0, PAD), pl.ds(rows - PAD, PAD)
@@ -140,7 +128,7 @@
         halo(9, pack.at[:, last, :], left_t, down, right),
     ]
 
-    for copy in (own[0], own[3], own[2]):
+    for copy in own[:2]:
         copy.wait()
     lane = lax.broadcasted_iota(jnp.int32, (rows, lanes), 1)
     for t in range(tiles):
@@ -157,19 +145,6 @@
         step *= 2
     pack[tiles] = acc
 
-    for copy in beside:
-        copy.start()
-
-    @pl.when(has_up)
-    def _():
-        for copy in to_up:
-            copy.start()
-
-    @pl.when(has_down)
-    def _():
-        for copy in to_down:
-            copy.start()
-
     @pl.when(jnp.logical_not(has_up))
     def _():
         for ref in (temp_t, spread_t, left_t, right_t):
@@ -179,6 +154,9 @@
     def _():
         for ref in (temp_b, spread_b, left_b, right_b):
             ref[...] = jnp.zeros_like(ref)
+
+    for copy in own[2:]:
+        copy.wait()
 
     xs[...] = jnp.zeros_like(xs)
     xs[0:levels, 0:hid] = w0t[0:levels, :] * 0.5
@@ -198,9 +176,43 @@
     bf_c[...] = column(bf[...])
     xs[...] = jnp.zeros_like(xs)
 
-    own[1].wait()
-    for copy in out:
-        copy.wait()
+    pl.semaphore_wait(
+        barrier, 2 + 3 * has_up.astype(jnp.int32) + 3 * has_down.astype(jnp.int32))
+
+    chunk = half // CHUNKS
+
+    def swap(i, src, dst):
+        return pltpu.make_async_remote_copy(
+            src_ref=src, dst_ref=dst, send_sem=send_sem.at[i], recv_sem=recv_sem.at[i],
+            device_id=at(partner, lon), device_id_type=MESH)
+
+    out = []
+    for c in range(CHUNKS):
+        theirs_c = pl.ds(pl.multiple_of(theirs + c * chunk, chunk), chunk)
+        here_c = pl.ds(c * chunk, chunk)
+        out.append([
+            swap(3 * c, temp.at[:, theirs_c, :], temp_r.at[:, here_c, :]),
+            swap(3 * c + 1, moist.at[:, theirs_c, :], moist_r.at[:, here_c, :]),
+            swap(3 * c + 2, mu.at[theirs_c, :], mu_r.at[here_c, :]),
+        ])
+
+    for copy in out[0] + beside:
+        copy.start()
+
+    @pl.when(has_up)
+    def _():
+        for copy in to_up:
+            copy.start()
+
+    @pl.when(has_down)
+    def _():
+        for copy in to_down:
+            copy.start()
+
+    for later in out[1:]:
+        for copy in later:
+            copy.start()
+
 
     temp_f = temp_v.reshape(levels * rows, lanes)
     moist_f = moist_v.reshape(levels * rows, lanes)
@@ -217,7 +229,12 @@
             send_sem=out_send.at[g], recv_sem=out_recv.at[g],
             device_id=at(partner, lon), device_id_type=MESH)
 
-    def network(g, carry):
+    heat_f = heat.reshape(levels * rows, lanes)
+
+    def place_row(r, value):
+        heat_f[pl.ds(r, levels, stride=rows), :] = value * lit[r].astype(jnp.float32)
+
+    def network(g, beside_it=lambda part: None):
         for j in range(GROUP):
             i = g * GROUP + j
             r = mine + i
@@ -233,16 +250,24 @@
             xs[2 * lp:2 * lp + 1, cols] = (
                 mu_v[pl.ds(r, 1), :] * on + mu_r[pl.ds(i, 1), :] * off)
         h = gate(dot3(w0_hi[...], w0_lo[...], xs[...]) + wide(b0_c[...]))
+        beside_it(0)
         for k in range(depth):
             h = gate(dot3(wm_hi[k], wm_lo[k], h) + wide(bm_c[k]))
+            beside_it(1 + k)
         y = dot3(wf_hi[...], wf_lo[...], h) + wide(bf_c[...])
         y = y * xs[2 * lp:2 * lp + 1, :]
         for j in range(GROUP):
-            res[g * GROUP + j] = y[:, j * lanes:(j + 1) * lanes]
+            value = y[:, j * lanes:(j + 1) * lanes]
+            res[g * GROUP + j] = value
+            place_row(mine + g * GROUP + j, value)
         send(g).start()
-        return carry
-
-    lax.fori_loop(0, half // GROUP, network, 0)
+
+    def arrive(c):
+        for copy in out[c]:
+            copy.wait()
+
+    arrive(0)
+    network(0)
 
     for copy in beside:
         copy.wait()
@@ -267,7 +292,7 @@
         return jnp.concatenate([top, middle, bottom], axis=0)
 
     def advance(x, f, west, east):
-        beside = roll(x, 1, 0) + roll(x, tall - 1, 0) + west + east
+        beside = roll(x, 1, 0) + roll(x, x.shape[0] - 1, 0) + west + east
         return x + f * (beside - 4.0 * x)
 
     slot = lax.broadcasted_iota(jnp.int32, (tall, lanes), 1)
@@ -288,29 +313,39 @@
         east = advance(east, f_east, roll(east, 1, 1), roll(east, lanes - 1, 1))
         edge_1[t] = jnp.where(place == 1, roll(east, lanes - 1, 1), roll(west, 1, 1))
 
-    f_all = stack(spread_t[...], spread_v[...], spread_b[...])
-    for k in range(levels):
-        t, m = divmod(k, slots)
+    f_all[...] = stack(spread_t[...], spread_v[...], spread_b[...])
+    def diffuse(k):
+        t, m = k // slots, lax.rem(k, slots)
         turn = lanes - 2 - EDGE * m
         x = stack(temp_t[k], temp_v[k], temp_b[k])
         for edge in (edge_0, edge_1):
-            rim = roll(edge[t], turn, 1)
+            rim = pltpu.roll(edge[t], turn, 1)
             west = jnp.where(slot == 0, rim, roll(x, 1, 1))
             east = jnp.where(slot == lanes - 1, rim, roll(x, lanes - 1, 1))
-            x = advance(x, f_all, west, east)
+            x = advance(x, f_all[...], west, east)
         nxt[k] = x[PAD:PAD + rows]
 
-    heat_f = heat.reshape(levels * rows, lanes)
-    nxt_f = nxt.reshape(levels * rows, lanes)
-
-    def place_row(r, value):
-        there = pl.ds(r, levels, stride=rows)
-        value = value * lit[r].astype(jnp.float32)
-        heat_f[there, :] = value
-        nxt_f[there, :] = nxt_f[there, :] + value
-
-    for i in range(half):
-        place_row(mine + i, res[i])
+    per = levels // (groups - 1)
+    parts = depth + 1
+
+    def both(g, carry):
+        @pl.when(g == groups // CHUNKS)
+        def _():
+            arrive(1)
+
+        begin = (g - 1) * per
+
+        def some(part):
+            for k in range(per * part // parts, per * (part + 1) // parts):
+                diffuse(begin + k)
+
+        network(g, some)
+        return carry
+
+    lax.fori_loop(1, groups, both, 0)
+    for k in range(per * (groups - 1), levels):
+        diffuse(jnp.int32(k))
+
     for g in range(half // GROUP):
         send(g).wait()
     for i in range(half):
@@ -329,7 +364,6 @@
     f32, bf16 = jnp.float32, jnp.bfloat16
     vmem = pl.BlockSpec(memory_space=pltpu.VMEM)
     hbm = pl.BlockSpec(memory_space=pltpu.HBM)
-    smem = pl.BlockSpec(memory_space=pltpu.SMEM)
     groups = half // GROUP
     dma = pltpu.SemaphoreType.DMA
 
@@ -339,9 +373,11 @@
     return pl.pallas_call(
         kernel,
         out_shape=(jax.ShapeDtypeStruct(temp.shape, f32),) * 2,
-        in_specs=[hbm, hbm, hbm, smem, hbm] + [vmem] * 6,
+        in_specs=[hbm] * 11,
         out_specs=(vmem, vmem),
         scratch_shapes=[
+            pltpu.SMEM((rows,), jnp.int32), buf(*w0.T.shape), buf(1, hid), buf(*wm.shape),
+            buf(*bm.shape), buf(*wf.shape), buf(1, levels),
             buf(levels, rows, lanes), buf(levels, rows, lanes), buf(rows, lanes), buf(rows, lanes),
             buf(levels, half, lanes), buf(levels, half, lanes), buf(half, lanes),
             buf(hid, kp, dtype=bf16), buf(hid, kp, dtype=bf16),
@@ -353,13 +389,16 @@
             buf(tiles + 1, rows, lanes),
             buf(tiles + 1, rows, lanes), buf(tiles + 1, PAD, lanes), buf(tiles + 1, PAD, lanes),
             buf(tiles + 1, rows, lanes), buf(tiles + 1, PAD, lanes), buf(tiles + 1, PAD, lanes),
-            buf(tiles, tall, lanes), buf(tiles, tall, lanes),
-            dma((4,)), dma((3,)), dma((3,)), dma((groups,)), dma((groups,)),
+            buf(tiles, tall, lanes), buf(tiles, tall, lanes), buf(tall, lanes),
+            dma((11,)), dma((3 * CHUNKS,)), dma((3 * CHUNKS,)), dma((groups,)), dma((groups,)),
             dma((10,)), dma((10,)),
         ],
         compiler_params=pltpu.CompilerParams(
             collective_id=0, has_side_effects=True, vmem_limit_bytes=48 << 20),
-    )(temp, moist, mu, lit, spread, w0.T, b0[None, :], wm, bm, wf, bf[None, :])
+    )(*(
+        pltpu.with_memory_space_constraint(x, pltpu.HBM)
+        for x in (temp, moist, mu, lit, spread, w0.T, b0[None, :], wm, bm, wf, bf[None, :])
+    ))
 
 
 def on_device(
@@ -375,7 +414,7 @@
     final_layer_matrix,
     final_layer_offset,
 ):
-    return tuple(run(
+    heating, state = run(
         thermal_departure,
         moisture_profile,
         solar_elevation_factor,
@@ -387,7 +426,8 @@
         inner_layer_offsets,
         final_layer_matrix,
         final_layer_offset,
-    ))
+    )
+    return heating, state + heating
 
 
 def solution(mesh):

time: 45.9 us -> 29.3 us (0.64)
  Pallas kernels: 35.2 us -> 25.9 us
  local copies, waits for them, and re-layouts: 9.61 us -> 1.11 us
  other arithmetic: 0 us -> 1.43 us
    pallas_call x1, Pallas kernels: 35.2 us -> 25.9 us  [run(): pl.pallas_call(kernel, out_shape=(jax.ShapeDtypeStruct(temp.shape, f32),)...]
    unnamed x20 -> x1, local copies, waits for them, and re-layouts: 9.61 us -> 1.11 us
    add x0 -> x1, other arithmetic: none -> 1.43 us  [on_device(): return (heating, state + heating)]
where the time goes in v3:
time: 29.3 us; the launch traced here: 29.1 us
  Pallas kernels  25.9 us (88%)
  other arithmetic  1.43 us (5%)
  local copies, waits for them, and re-layouts  1.11 us (4%)
  between operations  0.64 us (2%)
    pallas_call x1, Pallas kernels, run(): pl.pallas_call(kernel, out_shape=(jax.ShapeDtypeStruct(temp.shape, f32),)...  25.9 us
    add x1, other arithmetic, on_device(): return (heating, state + heating)  1.43 us
    unnamed x1, local copies, waits for them, and re-layouts  1.11 us

profile of v3, /device:TPU:0, one launch (start us, length us, event | category | flops | bytes accessed | tf_op | source)
XLA Modules:
  0.0 29.1 jit_solution(6183882452942289825)
XLA Ops:
  0.6 25.9 %shard_map.122 = (f32[90,32,128]{2,1,0:T(8,128)S(1)}, f32[90,32,128]{2,1,0:T(8,128)S(1)}) custom-call(f32[90,32,128]{2,1,0:T(8,128)} %temp.1, f32[90,32,128]{2,1,0:T(8,128)} %moist.1, f32[32,128]{1,0:T(8,128)} %mu.1, s32[32]{0:T(128)} %bitcast.6, f32[32,128]{1,0:T(8,128)} %spread.1, f32[181,512]{1,0:T(8,128)} %bitcast.4, f32[1,512]{1,0:T(1,128)} %bitcast.5, ...), custom_call_target="tpu_custom_call" | custom-call | tf_op jit(solution)/shard_map/pallas_call | solution.py:373
  26.6 1.4 %add.3 = f32[90,32,128]{2,1,0:T(8,128)} add(f32[90,32,128]{2,1,0:T(8,128)S(1)} %get-tuple-element.5, f32[90,32,128]{2,1,0:T(8,128)S(1)} %get-tuple-element.8) | non-fusion elementwise | flops 368640 | bytes 4423680 | tf_op jit(solution)/shard_map/add | solution.py:430
  28.0 1.1 %copy.14 = f32[90,32,128]{2,1,0:T(8,128)} copy(f32[90,32,128]{2,1,0:T(8,128)S(1)} %get-tuple-element.8) | data formatting | bytes 2949120

commit v4 on v3

--- a/solution.py
+++ b/solution.py
@@ -266,8 +266,12 @@
         for copy in out[c]:
             copy.wait()
 
+    early = groups // CHUNKS
     arrive(0)
-    network(0)
+    for g in range(early):
+        network(g)
+    for c in range(1, CHUNKS):
+        arrive(c)
 
     for copy in beside:
         copy.wait()
@@ -325,15 +329,11 @@
             x = advance(x, f_all[...], west, east)
         nxt[k] = x[PAD:PAD + rows]
 
-    per = levels // (groups - 1)
+    per = levels // (groups - early)
     parts = depth + 1
 
     def both(g, carry):
-        @pl.when(g == groups // CHUNKS)
-        def _():
-            arrive(1)
-
-        begin = (g - 1) * per
+        begin = (g - early) * per
 
         def some(part):
             for k in range(per * part // parts, per * (part + 1) // parts):
@@ -342,8 +342,8 @@
         network(g, some)
         return carry
 
-    lax.fori_loop(1, groups, both, 0)
-    for k in range(per * (groups - 1), levels):
+    lax.fori_loop(early, groups, both, 0)
+    for k in range(per * (groups - early), levels):
         diffuse(jnp.int32(k))
 
     for g in range(half // GROUP):

time: 29.3 us -> 31.4 us (1.072)
  Pallas kernels: 25.9 us -> 28.1 us
    pallas_call x1, Pallas kernels: 25.9 us -> 28.1 us  [run(): pl.pallas_call(kernel, out_shape=(jax.ShapeDtypeStruct(temp.shape, f32),)...]
where the time goes in v4:
time: 31.4 us; the launch traced here: 31.3 us
  Pallas kernels  28.1 us (89%)
  other arithmetic  1.43 us (5%)
  local copies, waits for them, and re-layouts  1.11 us (4%)
  between operations  0.64 us (2%)
    pallas_call x1, Pallas kernels, run(): pl.pallas_call(kernel, out_shape=(jax.ShapeDtypeStruct(temp.shape, f32),)...  28.1 us
    add x1, other arithmetic, on_device(): return (heating, state + heating)  1.43 us
    unnamed x1, local copies, waits for them, and re-layouts  1.11 us

profile of v4, /device:TPU:0, one launch (start us, length us, event | category | flops | bytes accessed | tf_op | source)
XLA Modules:
  0.0 31.3 jit_solution(3288688903235779402)
XLA Ops:
  0.6 28.1 %shard_map.122 = (f32[90,32,128]{2,1,0:T(8,128)S(1)}, f32[90,32,128]{2,1,0:T(8,128)S(1)}) custom-call(f32[90,32,128]{2,1,0:T(8,128)} %temp.1, f32[90,32,128]{2,1,0:T(8,128)} %moist.1, f32[32,128]{1,0:T(8,128)} %mu.1, s32[32]{0:T(128)} %bitcast.6, f32[32,128]{1,0:T(8,128)} %spread.1, f32[181,512]{1,0:T(8,128)} %bitcast.4, f32[1,512]{1,0:T(1,128)} %bitcast.5, ...), custom_call_target="tpu_custom_call" | custom-call | tf_op jit(solution)/shard_map/pallas_call | solution.py:373
  28.7 1.4 %add.3 = f32[90,32,128]{2,1,0:T(8,128)} add(f32[90,32,128]{2,1,0:T(8,128)S(1)} %get-tuple-element.5, f32[90,32,128]{2,1,0:T(8,128)S(1)} %get-tuple-element.8) | non-fusion elementwise | flops 368640 | bytes 4423680 | tf_op jit(solution)/shard_map/add | solution.py:430
  30.2 1.1 %copy.14 = f32[90,32,128]{2,1,0:T(8,128)} copy(f32[90,32,128]{2,1,0:T(8,128)S(1)} %get-tuple-element.8) | data formatting | bytes 2949120
